TPU v7x, 32 devices: a whole 2x2x4 slice. The times are simulated.
32 devices in a mesh: ctx: 8 (over z, y), fsdp: 4 (over x, core).
Axes of the slice: x: 2, y: 2, z: 4, core: 2. Of those that a mesh axis runs over, the one named last changes fastest.
Arguments:
- tokens: bfloat16 [4, 1024, 2048], P('fsdp', 'ctx'), may hold values from -6 to 6
- cotangent: bfloat16 [4, 1024, 2048], P('fsdp', 'ctx'), may hold values from -6 to 6
- pair_table: int32 [8], replicated, may hold values from 0 to 7, each once
- doc_lengths: int32 [4, 3], P('fsdp'), may hold values from 1 to 512, 1024 in all within a row
- attn_gain: bfloat16 [2048], P('fsdp'), may hold values from 0.099609375 to 1.8984375
- query_weight: bfloat16 [2048, 2048], P('fsdp'), may hold values from -0.125 to 0.125
- key_matrix: bfloat16 [2048, 512], P('fsdp'), may hold values from -0.125 to 0.125
- value_matrix: bfloat16 [2048, 512], P('fsdp'), may hold values from -0.125 to 0.125
- output_weight: bfloat16 [2048, 2048], P('fsdp'), may hold values from -1 to 1
- mlp_gain: bfloat16 [2048], P('fsdp'), may hold values from 0.099609375 to 1.8984375
- gate_weight: bfloat16 [2048, 8192], P('fsdp'), may hold values from -0.125 to 0.125
- up_weight: bfloat16 [2048, 8192], P('fsdp'), may hold values from -0.125 to 0.125
- down_weight: bfloat16 [8192, 2048], P('fsdp'), may hold values from -0.0625 to 0.0625
Outputs:
- output: bfloat16 [4, 1024, 2048], P('fsdp', 'ctx')
- input_grad: bfloat16 [4, 1024, 2048], P('fsdp', 'ctx')
- attn_gain_grad: float32 [2048], P(('ctx', 'fsdp'))
- query_weight_grad: float32 [2048, 2048], P(('ctx', 'fsdp'))
- key_weight_grad: float32 [2048, 512], P(('ctx', 'fsdp'))
- value_weight_grad: float32 [2048, 512], P(('ctx', 'fsdp'))
- output_weight_grad: float32 [2048, 2048], P(('ctx', 'fsdp'))
- mlp_gain_grad: float32 [2048], P(('ctx', 'fsdp'))
- gate_weight_grad: float32 [2048, 8192], P(('ctx', 'fsdp'))
- up_weight_grad: float32 [2048, 8192], P(('ctx', 'fsdp'))
- down_weight_grad: float32 [8192, 2048], P(('ctx', 'fsdp'))
Inputs may be any that keep to these rules, and one draw needn't show every extreme that they name: `pair_table`: each index of ctx appears exactly once. `doc_lengths`: the 3 documents of a sequence fill its 1024 positions in order; in every sequence one document has exactly 512 positions.
All inputs are finite; a program needn't handle non-finite values.
Results may differ from a plain program's by a relative error of at most 0.017.
Values may be sent and summed in bfloat16 or wider, within the bound.
No kernel may reach another device: no remote copies, remote signals or barrier semaphores. Data moves between devices by JAX's collectives and lax.ppermute only.
A program may use at most 512 MiB of HBM per device.

v0:
```python
import math

import jax
import jax.numpy as jnp
from jax import lax
from jax.sharding import Mesh
from jax.sharding import PartitionSpec as P


MODEL_WIDTH = 2048
QUERY_HEADS = 32
KEY_VALUE_HEADS = 8
HEAD_SIZE = 64


epsilon = 1e-05
masked_score = -1e30


def rms_forward(values_in, norm_gain):
    scale_row = lax.rsqrt(jnp.mean(values_in * values_in, axis=-1, keepdims=True) + epsilon)
    return (values_in * scale_row * norm_gain, scale_row)


def rms_backward(values_in, scale_row, norm_gain, grad_normed):
    weighted = grad_normed * norm_gain
    inner_sum = jnp.mean(weighted * values_in, axis=-1, keepdims=True)
    grad_values = scale_row * weighted - values_in * scale_row * scale_row * scale_row * inner_sum
    grad_gain = jnp.sum(grad_normed * values_in * scale_row, axis=0)
    return (grad_values, grad_gain)


def rope_tables(rot_places, half_dim):
    frequency = 1.0 / 500000.0 ** (jnp.arange(half_dim, dtype=jnp.float32) * 2.0 / (2 * half_dim))
    angles = rot_places.astype(jnp.float32)[..., None] * frequency
    return (jnp.cos(angles), jnp.sin(angles))


def apply_rotation(vectors, cosine_table, sine_table):
    half_dim = vectors.shape[-1] // 2
    front_half = vectors[..., :half_dim]
    back_half = vectors[..., half_dim:]
    cos_heads = cosine_table[..., None, :]
    sin_heads = sine_table[..., None, :]
    return jnp.concatenate(
        [
            front_half * cos_heads - back_half * sin_heads,
            back_half * cos_heads + front_half * sin_heads,
        ],
        axis=-1,
    )


def inverse_rotation(vectors, cosine_table, sine_table):
    half_dim = vectors.shape[-1] // 2
    front_half = vectors[..., :half_dim]
    back_half = vectors[..., half_dim:]
    cos_heads = cosine_table[..., None, :]
    sin_heads = sine_table[..., None, :]
    return jnp.concatenate(
        [
            front_half * cos_heads + back_half * sin_heads,
            back_half * cos_heads - front_half * sin_heads,
        ],
        axis=-1,
    )


def layout_places(pair_table, block_len, sequence_length):
    row_ids = jnp.arange(sequence_length, dtype=jnp.int32)
    shard_ids = row_ids // (2 * block_len)
    within = row_ids % (2 * block_len)
    num_devices = pair_table.shape[0]
    device_ids = jnp.arange(num_devices, dtype=jnp.int32)
    chosen = jnp.sum(
        jnp.where(shard_ids[:, None] == device_ids[None, :], pair_table[None, :], 0), axis=1
    )
    block_ids = jnp.where(within < block_len, chosen, 2 * num_devices - 1 - chosen)
    return block_ids * block_len + within % block_len


def document_places(places, lengths_row):
    doc_ends = jnp.cumsum(lengths_row)
    doc_starts = doc_ends - lengths_row
    doc_ids = jnp.sum((places[:, None] >= doc_ends[None, :]).astype(jnp.int32), axis=1)
    doc_numbers = jnp.arange(lengths_row.shape[0], dtype=jnp.int32)
    picked = jnp.sum(
        jnp.where(doc_ids[:, None] == doc_numbers[None, :], doc_starts[None, :], 0), axis=1
    )
    return (doc_ids, places - picked)


EVERY = ("c", "x", "k")
CHIPS = ("c", "x")


class Wires:
    def __init__(self, ctx_count):
        self.count = ctx_count
        self.total = ctx_count * 4
        self.paths = ctx_count == 8
        self.c = lax.axis_index("c")
        self.x = lax.axis_index("x")
        self.k = lax.axis_index("k")
        if self.paths:
            z_of = lambda i: i >> 3
            middle = [i for i in range(32) if z_of(i) in (1, 2)]
            ends = [i for i in range(32) if z_of(i) in (0, 3)]
            self.mid = [(i, i ^ 24) for i in middle]
            self.outward = [(i, i ^ 8) for i in middle]
            self.inward = [(i, i ^ 8) for i in ends]
            z_index = self.c // 2
            self.inner = (z_index == 1) | (z_index == 2)

    def swap(self, value, bits):
        return lax.ppermute(value, EVERY, [(i, i ^ bits) for i in range(self.total)])

    def send(self, value, pairs):
        return lax.ppermute(value, EVERY, pairs)

    def over_fsdp(self, shard):
        other = self.swap(shard, 2)
        near = self.x == 0
        both = jnp.stack([jnp.where(near, shard, other), jnp.where(near, other, shard)])
        partner = self.swap(both, 1)
        first = self.k == 0
        even = jnp.where(first, both, partner)
        odd = jnp.where(first, partner, both)
        return jnp.stack([even, odd], axis=1).reshape((-1,) + shard.shape[1:])

    def fsdp_slots(self, shard):
        other = self.swap(shard, 2)
        return [shard, self.swap(shard, 1), other, self.swap(other, 1)]

    def fsdp_reslot(self, value):
        grid = value.reshape(value.shape[:-1] + (2, 2, value.shape[-1] // 4))
        axis = value.ndim - 1
        grid = jnp.where(self.x == 1, jnp.flip(grid, axis), grid)
        grid = jnp.where(self.k == 1, jnp.flip(grid, axis + 1), grid)
        return grid.reshape(value.shape)

    def sum_fsdp(self, parts, axis):
        grid = jnp.moveaxis(parts, axis, 0)
        grid = grid.reshape((2, 2) + grid.shape[1:])
        mine = lax.dynamic_index_in_dim(grid, self.k, 1, keepdims=False)
        theirs = lax.dynamic_index_in_dim(grid, 1 - self.k, 1, keepdims=False)
        pair_sum = mine + self.swap(theirs, 1)
        mine = lax.dynamic_index_in_dim(pair_sum, self.x, 0, keepdims=False)
        theirs = lax.dynamic_index_in_dim(pair_sum, 1 - self.x, 0, keepdims=False)
        return mine + self.swap(theirs, 2)

    def ctx_gather(self, value):
        return lax.all_gather(value, "c", axis=0, tiled=False)

    def ctx_slots(self, value):
        half = value.shape[0] // 2
        if not self.paths:
            found = self.ctx_gather(value)
            return [found[:, :half], found[:, half:]]
        upper = self.z_spread(value[:half])
        lower = jnp.stack([value[half:], self.swap(value[half:], 4)])
        lower = self.z_spread(lower).reshape(self.count, half, -1)
        upper = jnp.stack([upper, self.swap(upper, 4)], axis=1).reshape(self.count, half, -1)
        return [upper, lower]

    def reslot(self, value, axis):
        if not self.paths:
            return value
        shape = value.shape
        value = value.reshape(shape[:axis] + (2, 2, 2) + shape[axis + 1 :])
        for step in range(3):
            value = jnp.where((self.c >> (2 - step)) & 1 == 1, jnp.flip(value, axis + step), value)
        return value.reshape(shape)

    def z_spread(self, value):
        step = self.swap(value, 8)
        over = self.send(value, self.mid)
        over_step = self.send(step, self.mid)
        out = self.send(over, self.outward)
        out_step = self.send(over_step, self.outward)
        second = jnp.where(self.inner, over_step, out)
        third = jnp.where(self.inner, over, out_step)
        return jnp.stack([value, step, second, third])

    def z_collect(self, parts):
        own, near, far, across = parts[0], parts[1], parts[2], parts[3]
        low = jnp.bfloat16
        wide = jnp.float32
        got = self.send(jnp.stack([far, across]).astype(low), self.inward).astype(wide)
        across = across + got[0]
        far = far + got[1]
        got = self.send(jnp.stack([across, far]).astype(low), self.mid).astype(wide)
        own = own + got[0]
        near = near + got[1]
        return own + self.swap(near.astype(low), 8).astype(wide)

    def spread(self, value):
        if not self.paths:
            return [lax.all_gather(value, CHIPS, axis=0, tiled=True)]
        half = value.shape[0] // 2
        width = value.shape[1]
        found = []
        for rows, order in ((value[:half], (4, 2)), (value[half:], (2, 4))):
            held = self.z_spread(rows)
            for bits in order:
                held = jnp.stack([held, self.swap(held, bits)])
            found.append(held.reshape(16 * half, width))
        return found

    def spread_late(self, value):
        if not self.paths:
            return self.spread(value)
        half = value.shape[0] // 2
        width = value.shape[1]
        held = lax.all_gather(value, CHIPS, axis=0, tiled=False)
        held = held.reshape(2, 2, 2, 2, 2, half, width)
        bits = ((self.c >> 2) & 1, (self.c >> 1) & 1, self.c & 1, self.x)
        for step, bit in enumerate(bits):
            held = jnp.where(bit == 1, jnp.flip(held, step), held)
        return [
            held[:, :, :, :, part].transpose(order).reshape(16 * half, width)
            for part, order in enumerate(((3, 2, 0, 1, 4, 5), (2, 3, 0, 1, 4, 5)))
        ]

    def collect(self, parts):
        if not self.paths:
            low = parts[0].astype(jnp.bfloat16)
            return lax.psum_scatter(low, CHIPS, scatter_dimension=0, tiled=True).astype(jnp.float32)
        found = []
        for part, order in zip(parts, ((2, 4), (4, 2))):
            half = part.shape[0] // 16
            held = part.reshape(2, 2, 4, half, part.shape[1])
            for bits in order:
                held = held[0] + self.swap(held[1].astype(jnp.bfloat16), bits).astype(jnp.float32)
            found.append(self.z_collect(held))
        return jnp.concatenate(found, axis=0)


def body(
    tokens,
    cotangent,
    pair_table,
    doc_lengths,
    attn_gain,
    query_weight,
    key_matrix,
    value_matrix,
    output_weight,
    mlp_gain,
    gate_weight,
    up_weight,
    down_weight,
):
    low = jnp.bfloat16
    wide = jnp.float32
    ctx_count = lax.axis_size("c")
    wires = Wires(ctx_count)
    shard_length = tokens.shape[1]
    block_len = shard_length // 2
    length = shard_length * ctx_count
    c, x, k = wires.c, wires.x, wires.k
    heads = QUERY_HEADS // ctx_count
    head_width = heads * HEAD_SIZE
    share = max(1, ctx_count // KEY_VALUE_HEADS)
    kv_index = c // share
    kv_part = HEAD_SIZE // share
    hidden_total = gate_weight.shape[1]
    hidden_chip = hidden_total // (2 * ctx_count)
    score_scale = 1.0 / math.sqrt(HEAD_SIZE)

    def mm(left, right):
        return jnp.dot(left, right, preferred_element_type=wide)

    def mm_t(left, right):
        return jnp.einsum("ij,kj->ik", left, right, preferred_element_type=wide)

    def t_mm(left, right):
        return jnp.einsum("ti,tj->ij", left, right, preferred_element_type=wide)

    places = layout_places(pair_table, block_len, length).reshape(ctx_count, 2, block_len)
    places = wires.reslot(places, 0).transpose(1, 0, 2).reshape(length)
    docs, rot = document_places(places, doc_lengths[0])
    cosine_table, sine_table = rope_tables(rot, HEAD_SIZE // 2)

    own = tokens[0]
    own_wide = own.astype(wide)
    dy = cotangent[0]

    row_slots = wires.ctx_slots(own)
    gains = wires.over_fsdp(jnp.stack([attn_gain, mlp_gain], axis=1)).astype(wide)
    attn_gain_f = gains[:, 0]
    mlp_gain_f = gains[:, 1]
    take = lambda array, start, size: lax.dynamic_slice_in_dim(array, start, size, axis=1)
    head_shard = jnp.concatenate(
        [
            take(query_weight, c * head_width, head_width),
            take(key_matrix, kv_index * HEAD_SIZE, HEAD_SIZE),
            take(value_matrix, kv_index * HEAD_SIZE, HEAD_SIZE),
        ],
        axis=1,
    )
    head_weights = wires.over_fsdp(head_shard)
    output_slots = wires.fsdp_slots(output_weight)

    def parts_of(value):
        return jnp.split(value, 4, axis=-1)

    def from_slots(pieces):
        return wires.fsdp_reslot(jnp.concatenate(pieces, axis=-1))

    normed_one = jnp.concatenate(
        [
            rms_forward(half.reshape(-1, MODEL_WIDTH).astype(wide), attn_gain_f)[0].astype(low)
            for half in row_slots
        ]
    )

    def to_rows(value):
        value = wires.reslot(value.reshape(2, ctx_count, block_len, -1), 1)
        return value.transpose(1, 0, 2, 3).reshape(length, -1)

    def from_rows(value):
        value = value.reshape(ctx_count, 2, block_len, -1).transpose(1, 0, 2, 3)
        return wires.reslot(value, 1).reshape(length, -1)

    dy_all = wires.spread_late(dy)
    projected = mm(normed_one, head_weights)
    q_rot = apply_rotation(
        projected[:, :head_width].reshape(length, heads, HEAD_SIZE), cosine_table, sine_table
    ).astype(low)
    k_rot = apply_rotation(
        projected[:, None, head_width : head_width + HEAD_SIZE], cosine_table, sine_table
    ).astype(low)[:, 0]
    v_low = projected[:, head_width + HEAD_SIZE :].astype(low)
    allowed = (places[None, :] <= places[:, None]) & (docs[None, :] == docs[:, None])

    def scores_of(queries):
        raw = jnp.einsum("rhd,ld->hrl", queries, k_rot, preferred_element_type=wide) * score_scale
        return jnp.where(allowed[None], raw, masked_score)

    scores = scores_of(q_rot)
    row_max = jnp.max(scores, axis=2, keepdims=True)
    exponent = jnp.exp(scores - row_max)
    row_total = jnp.sum(exponent, axis=2, keepdims=True)
    probs = exponent / row_total
    probs_low = probs.astype(low)
    mixed = (
        jnp.einsum("hrl,ld->rhd", probs_low, v_low, preferred_element_type=wide)
        .astype(low)
        .reshape(length, head_width)
    )
    mixed = to_rows(mixed)
    mixed_rows = lax.all_to_all(mixed, "c", 0, 1, tiled=True)
    hidden = own_wide
    for piece, slot in zip(parts_of(wires.fsdp_reslot(mixed_rows)), output_slots):
        hidden = hidden + mm(piece, slot)
    normed_two, scale_two = rms_forward(hidden, mlp_gain_f)
    normed_two = normed_two.astype(low)

    def chip_columns(weight):
        start = hidden_chip * 2 * c
        mine = take(weight, start + hidden_chip * x, hidden_chip)
        theirs = take(weight, start + hidden_chip * (1 - x), hidden_chip)
        other = wires.swap(theirs, 2)
        near = x == 0
        both = jnp.stack([jnp.where(near, mine, other), jnp.where(near, other, mine)])
        partner = wires.swap(both, 1)
        first = k == 0
        even = jnp.where(first, both, partner)
        odd = jnp.where(first, partner, both)
        return jnp.stack([even, odd], axis=1).reshape(MODEL_WIDTH, hidden_chip)

    gate_chip = chip_columns(gate_weight)
    up_chip = chip_columns(up_weight)
    down_shard = down_weight.shape[0]
    holder = (2 * hidden_chip * c) // down_shard
    inside = 2 * hidden_chip * c - holder * down_shard
    down_mine = lax.dynamic_slice_in_dim(down_weight, inside + hidden_chip * x, hidden_chip)
    down_theirs = lax.dynamic_slice_in_dim(down_weight, inside + hidden_chip * (1 - x), hidden_chip)
    crossing = []
    for place in range(ctx_count):
        source = (2 * hidden_chip * place) // down_shard
        crossing.append((place * 4 + source, place * 4 + (source ^ 2)))
    down_other = wires.send(down_theirs, crossing)
    down_held = jnp.where(holder // 2 == x, down_mine, down_other)
    down_chip = jnp.where(holder % 2 == k, down_held, wires.swap(down_held, 1))

    normed_all = wires.spread(normed_two)
    kept = []
    grad_parts = []
    for normed_rows, dy_rows in zip(normed_all, dy_all):
        gate_proj = mm(normed_rows, gate_chip)
        up_proj = mm(normed_rows, up_chip)
        sigmoid_gate = jax.nn.sigmoid(gate_proj)
        silu_gate = gate_proj * sigmoid_gate
        activated = (silu_gate * up_proj).astype(low)
        grad_act = mm_t(dy_rows, down_chip)
        grad_up = (grad_act * silu_gate).astype(low)
        grad_gate = (
            grad_act * up_proj * sigmoid_gate * (1.0 + gate_proj * (1.0 - sigmoid_gate))
        ).astype(low)
        grad_parts.append(
            (mm_t(grad_gate, gate_chip) + mm_t(grad_up, up_chip)).astype(low)
        )
        kept.append((activated, grad_gate, grad_up))
    out_parts = [mm(activated, down_chip).astype(low) for activated, _, _ in kept]
    gate_term = 0.0
    up_term = 0.0
    down_term = 0.0
    for normed_rows, dy_rows, (activated, grad_gate, grad_up) in zip(normed_all, dy_all, kept):
        gate_term = gate_term + t_mm(normed_rows, grad_gate)
        up_term = up_term + t_mm(normed_rows, grad_up)
        down_term = down_term + t_mm(activated, dy_rows)
    normed_term = wires.collect(grad_parts)
    branch = wires.collect(out_parts)
    output = (hidden + branch).astype(low).reshape(tokens.shape)

    def core_sum(parts, axis):
        mine = lax.dynamic_index_in_dim(parts, k, axis, keepdims=False)
        theirs = lax.dynamic_index_in_dim(parts, 1 - k, axis, keepdims=False)
        return mine + wires.swap(theirs, 1)

    down_out = core_sum(down_term.reshape(2, hidden_chip // 2, MODEL_WIDTH), 0)
    row_count = MODEL_WIDTH // (4 * ctx_count)

    def columns_out(term):
        parts = core_sum(term.reshape(2 * ctx_count, 2, row_count, hidden_chip), 1)
        moved = lax.all_to_all(parts.astype(low), CHIPS, 0, 0, tiled=True)
        return moved.transpose(1, 0, 2).reshape(row_count, hidden_total).astype(wide)

    gate_out = columns_out(gate_term)
    up_out = columns_out(up_term)

    grad_hidden_part, mlp_gain_grad = rms_backward(hidden, scale_two, mlp_gain_f, normed_term)
    grad_hidden = dy.astype(wide) + grad_hidden_part
    grad_branch = grad_hidden.astype(low)
    grad_mixed_rows = from_slots([mm_t(grad_branch, slot).astype(low) for slot in output_slots])
    grad_mixed = lax.all_to_all(grad_mixed_rows, "c", 1, 0, tiled=True)
    branch_rows = wires.ctx_gather(grad_branch).reshape(length, MODEL_WIDTH)
    output_term = t_mm(mixed, branch_rows)
    output_out = wires.sum_fsdp(output_term.reshape(4, row_count, MODEL_WIDTH), 0)

    grad_heads = from_rows(grad_mixed).reshape(length, heads, HEAD_SIZE)
    grad_probs = jnp.einsum("rhd,ld->hrl", grad_heads, v_low, preferred_element_type=wide)
    inner_sum = jnp.sum(probs * grad_probs, axis=2, keepdims=True)
    grad_scores = (probs * (grad_probs - inner_sum)).astype(low)
    grad_q_rot = (
        jnp.einsum("hrl,ld->rhd", grad_scores, k_rot, preferred_element_type=wide) * score_scale
    )
    grad_k_rot = (
        jnp.einsum("hrl,rhd->ld", grad_scores, q_rot, preferred_element_type=wide) * score_scale
    )
    grad_v = jnp.einsum("hrl,rhd->ld", probs_low, grad_heads, preferred_element_type=wide)
    if share > 1:
        groups = [
            [(base * share + i) for i in range(share)] for base in range(ctx_count // share)
        ]
        both = lax.all_gather(
            jnp.stack([grad_k_rot, grad_v]), "c", axis=0, axis_index_groups=groups
        )
        both = jnp.sum(both, axis=0)
        grad_k_rot, grad_v = both[0], both[1]
    query_grad = (
        inverse_rotation(grad_q_rot, cosine_table, sine_table)
        .astype(low)
        .reshape(length, head_width)
    )
    key_grad = inverse_rotation(grad_k_rot[:, None], cosine_table, sine_table).astype(low)[:, 0]
    value_grad = grad_v.astype(low)
    if share > 1:
        key_grad = take(key_grad, (c % share) * kv_part, kv_part)
        value_grad = take(value_grad, (c % share) * kv_part, kv_part)
    packed = jnp.concatenate([query_grad, key_grad, value_grad], axis=1)
    packed_width = head_width + 2 * kv_part

    def unpack(rows_in):
        grid = rows_in.reshape(rows_in.shape[0], ctx_count, packed_width)
        flat = lambda piece: piece.reshape(rows_in.shape[0], -1)
        return (
            flat(grid[:, :, :head_width]),
            flat(grid[:, :, head_width : head_width + kv_part]),
            flat(grid[:, :, head_width + kv_part :]),
        )

    own_grads = unpack(lax.all_to_all(to_rows(packed), "c", 0, 1, tiled=True))
    late_slots = [wires.fsdp_slots(w) for w in (query_weight, key_matrix, value_matrix)]
    grad_normed_one = from_slots(
        [
            mm_t(own_grads[0], late_slots[0][slot])
            + mm_t(own_grads[1], late_slots[1][slot])
            + mm_t(own_grads[2], late_slots[2][slot])
            for slot in range(4)
        ]
    )
    scale_one = lax.rsqrt(jnp.mean(own_wide * own_wide, axis=-1, keepdims=True) + epsilon)
    grad_input_part, attn_gain_grad = rms_backward(
        own_wide, scale_one, attn_gain_f, grad_normed_one
    )
    input_grad = (grad_hidden + grad_input_part).astype(low).reshape(tokens.shape)

    packed_term = t_mm(normed_one, packed).reshape(ctx_count, 4, row_count, packed_width)
    packed_term = wires.sum_fsdp(packed_term, 1)
    packed_term = lax.all_to_all(packed_term, "c", 0, 0, tiled=True)
    query_out, key_out, value_out = unpack(
        packed_term.transpose(1, 0, 2).reshape(row_count, ctx_count * packed_width)
    )

    gain_parts = jnp.stack([attn_gain_grad, mlp_gain_grad]).reshape(2, 4 * ctx_count, row_count)
    gain_parts = lax.all_to_all(gain_parts.transpose(1, 0, 2), EVERY, 0, 0, tiled=True)
    gain_out = jnp.sum(gain_parts, axis=0)
    return (
        output,
        input_grad,
        gain_out[0],
        query_out,
        key_out,
        value_out,
        output_out,
        gain_out[1],
        gate_out,
        up_out,
        down_out,
    )


def solution(mesh):
    fsdp = ("x", "k")
    spread_all = ("c", "x", "k")
    ctx_count = mesh.shape["ctx"]
    grid = Mesh(mesh.devices.reshape(ctx_count, 2, 2), ("c", "x", "k"))
    row = P(fsdp, None)
    out_row = P(spread_all, None)
    act = P(fsdp, "c", None)
    return jax.shard_map(
        body,
        mesh=grid,
        in_specs=(act, act, P(), row, P(fsdp), row, row, row, row, P(fsdp), row, row, row),
        out_specs=(
            act,
            act,
            P(spread_all),
            out_row,
            out_row,
            out_row,
            out_row,
            P(spread_all),
            out_row,
            out_row,
            out_row,
        ),
        check_vma=False,
    )
```

profile of v0, /device:TPU:14, one launch (start us, length us, event | category | flops | bytes accessed | tf_op | source)
XLA Modules:
  0.0 908.1 jit_solution(15155926356207965791)
XLA Ops:
  9.6 4.6 collective-permute-start.2
  29.9 3.9 collective-permute-start.1
  36.5 23.9 %collective-permute-done.1 = bf16[64,2048]{1,0:T(8,128)(2,1)S(1)} collective-permute-done((bf16[64,2048]{1,0:T(8,128)(2,1)}, bf16[64,2048]{1,0:T(8,128)(2,1)S(1)}, u32[]{:S(2)}, u32[]{:S(2)}) %collective-permute-start.1) | collective-permute-done | bytes 262176 | tf_op jit(solution)/shard_map/ppermute | solution.py:119
  64.5 10.8 %collective-permute-done.4 = bf16[64,2048]{1,0:T(8,128)(2,1)S(1)} collective-permute-done((bf16[64,2048]{1,0:T(8,128)(2,1)S(1)}, bf16[64,2048]{1,0:T(8,128)(2,1)S(1)}, u32[]{:S(2)}, u32[]{:S(2)}) %collective-permute-start.4) | collective-permute-done | bytes 262176 | tf_op jit(solution)/shard_map/ppermute | solution.py:119
  75.3 4.4 collective-permute-start.12
  87.7 13.4 %collective-permute-done.12 = bf16[2,64,2048]{2,1,0:T(8,128)(2,1)S(1)} collective-permute-done((bf16[2,64,2048]{2,1,0:T(8,128)(2,1)S(1)}, bf16[2,64,2048]{2,1,0:T(8,128)(2,1)S(1)}, u32[]{:S(2)}, u32[]{:S(2)}) %collective-permute-start.12) | collective-permute-done | bytes 524320 | tf_op jit(solution)/shard_map/ppermute | solution.py:119
  101.2 16.5 %collective-permute-done.13 = bf16[2,64,2048]{2,1,0:T(8,128)(2,1)S(1)} collective-permute-done((bf16[2,64,2048]{2,1,0:T(8,128)(2,1)S(1)}, bf16[2,64,2048]{2,1,0:T(8,128)(2,1)S(1)}, u32[]{:S(2)}, u32[]{:S(2)}) %collective-permute-start.13) | collective-permute-done | bytes 524320 | tf_op jit(solution)/shard_map/ppermute | solution.py:119
  131.6 10.7 %fusion.160 = (f32[4,1024]{1,0:T(4,128)S(1)}, f32[4,1024,1024]{1,2,0:T(8,128)}) fusion(pred[1024,1024]{0,1:T(8,128)(4,1)} %compare_and_fusion, bf16[1024,4,32]{0,2,1:T(8,128)(2,1)S(1)} %get-tuple-element.59, bf16[1024,4,32]{0,2,1:T(8,128)(2,1)S(1)} %get-tuple-element.58, bf16[1024,32]{0,1:T(8,128)(2,1)S(1)} %get-tuple-element.86, ...), kind=kOutput, calls=%fused_computation.377 | convolution fusion | flops 554959872 | bytes 18497536 | tf_op jit(solution)/shard_map/sub | solution.py:343
  142.3 7.5 fusion.35
  155.0 9.7 %all-to-all-start = ((bf16[8,128,256]{2,1,0:T(8,128)(2,1)}), bf16[8,128,256]{2,1,0:T(8,128)(2,1)S(1)}, u32[]{:S(2)}, u32[]{:S(2)}) async-start(bf16[8,128,256]{2,1,0:T(8,128)(2,1)} %bitcast.44), calls=%async_computation | async-start | bytes 1048576 | tf_op jit(solution)/shard_map/all_to_all | solution.py:353
  215.1 3.8 collective-permute-done.23
  230.4 12.0 %collective-permute-done.24 = bf16[4,64,2048]{2,1,0:T(8,128)(2,1)S(1)} collective-permute-done((bf16[4,64,2048]{2,1,0:T(8,128)(2,1)S(1)}, bf16[4,64,2048]{2,1,0:T(8,128)(2,1)S(1)}, u32[]{:S(2)}, u32[]{:S(2)}) %collective-permute-start.24) | collective-permute-done | bytes 1048608 | tf_op jit(solution)/shard_map/ppermute | solution.py:116
  250.4 3.9 fusion.147
  268.0 24.6 %collective-permute-done.25 = bf16[2,4,64,2048]{3,2,1,0:T(8,128)(2,1)} collective-permute-done((bf16[2,4,64,2048]{3,2,1,0:T(8,128)(2,1)}, bf16[2,4,64,2048]{3,2,1,0:T(8,128)(2,1)}, u32[]{:S(2)}, u32[]{:S(2)}) %collective-permute-start.25) | collective-permute-done | bytes 2097184 | tf_op jit(solution)/shard_map/ppermute | solution.py:116
  299.0 3.7 fusion.162
  302.7 3.6 fusion.161
  306.3 3.6 fusion.164
  310.0 3.8 fusion.163
  313.8 14.6 %reverse_select_fusion.3 = bf16[2,2,2,2,2,64,2048]{6,5,4,3,2,1,0:T(8,128)(2,1)} fusion(bf16[2,2,2,2,2,64,2048]{6,5,4,3,2,1,0:T(8,128)(2,1)} %bitcast.477, pred[]{:T(512)S(6)} %eq.55), kind=kLoop, calls=%fused_computation.12 | loop fusion | flops 4194304 | bytes 16777216 | tf_op jit(solution)/shard_map/jit(_where)/select_n | solution.py:219
  328.3 14.6 %reverse_select_fusion.2 = bf16[2,2,2,2,2,64,2048]{6,5,4,3,2,1,0:T(8,128)(2,1)} fusion(bf16[2,2,2,2,2,64,2048]{6,5,4,3,2,1,0:T(8,128)(2,1)} %reverse_select_fusion.3, pred[]{:T(512)S(6)} %eq.54), kind=kLoop, calls=%fused_computation.11 | loop fusion | flops 4194304 | bytes 16777216 | tf_op jit(solution)/shard_map/jit(_where)/select_n | solution.py:219
  342.9 14.9 %reverse_select_fusion.1 = bf16[2,2,2,2,2,64,2048]{6,5,4,3,2,1,0:T(8,128)(2,1)} fusion(bf16[2,2,2,2,2,64,2048]{6,5,4,3,2,1,0:T(8,128)(2,1)} %reverse_select_fusion.2, pred[]{:T(512)S(6)} %eq.126), kind=kLoop, calls=%fused_computation.10 | loop fusion | flops 4194304 | bytes 16777216 | tf_op jit(solution)/shard_map/jit(_where)/select_n | solution.py:219
  357.8 14.6 %reverse_select_fusion = bf16[2,2,2,2,2,64,2048]{6,5,4,3,2,1,0:T(8,128)(2,1)} fusion(bf16[2,2,2,2,2,64,2048]{6,5,4,3,2,1,0:T(8,128)(2,1)} %reverse_select_fusion.1, pred[]{:T(512)S(6)} %eq.52), kind=kLoop, calls=%fused_computation.9 | loop fusion | flops 4194304 | bytes 16777216 | tf_op jit(solution)/shard_map/jit(_where)/select_n | solution.py:219
  372.4 3.8 slice_bitcast_fusion.1
  382.3 4.5 fusion.176
  396.2 4.7 fusion.175
  403.4 5.8 fusion.165
  422.9 7.5 add_convert_fusion.1
  433.2 5.8 fusion.166
  439.0 5.8 add_convert_fusion
  448.6 14.2 %collective-permute-done.32 = bf16[2,4,64,2048]{3,2,1,0:T(8,128)(2,1)} collective-permute-done((bf16[2,4,64,2048]{3,2,1,0:T(8,128)(2,1)}, bf16[2,4,64,2048]{3,2,1,0:T(8,128)(2,1)}, u32[]{:S(2)}, u32[]{:S(2)}) %collective-permute-start.32) | collective-permute-done | bytes 2097184 | tf_op jit(solution)/shard_map/ppermute | solution.py:116
  469.9 37.8 %collective-permute-done.49 = bf16[2,4,64,2048]{3,2,1,0:T(8,128)(2,1)} collective-permute-done((bf16[2,4,64,2048]{3,2,1,0:T(8,128)(2,1)}, bf16[2,4,64,2048]{3,2,1,0:T(8,128)(2,1)}, u32[]{:S(2)}, u32[]{:S(2)}) %collective-permute-start.49) | collective-permute-done | bytes 2097184 | tf_op jit(solution)/shard_map/ppermute | solution.py:116
  515.0 17.8 %collective-permute-done.33 = bf16[4,64,2048]{2,1,0:T(8,128)(2,1)S(1)} collective-permute-done((bf16[4,64,2048]{2,1,0:T(8,128)(2,1)S(1)}, bf16[4,64,2048]{2,1,0:T(8,128)(2,1)S(1)}, u32[]{:S(2)}, u32[]{:S(2)}) %collective-permute-start.33) | collective-permute-done | bytes 1048608 | tf_op jit(solution)/shard_map/ppermute | solution.py:116
  533.6 5.0 collective-permute-done.45
  540.1 13.5 %collective-permute-done.50 = bf16[4,64,2048]{2,1,0:T(8,128)(2,1)S(1)} collective-permute-done((bf16[4,64,2048]{2,1,0:T(8,128)(2,1)S(1)}, bf16[4,64,2048]{2,1,0:T(8,128)(2,1)S(1)}, u32[]{:S(2)}, u32[]{:S(2)}) %collective-permute-start.50) | collective-permute-done | bytes 1048608 | tf_op jit(solution)/shard_map/ppermute | solution.py:116
  555.2 4.5 collective-permute-done.55
  561.5 8.4 collective-permute-done.34
  571.3 9.7 %collective-permute-done.46 = bf16[2,64,2048]{2,1,0:T(8,128)(2,1)S(1)} collective-permute-done((bf16[2,64,2048]{2,1,0:T(8,128)(2,1)S(1)}, bf16[2,64,2048]{2,1,0:T(8,128)(2,1)S(1)}, u32[]{:S(2)}, u32[]{:S(2)}) %collective-permute-start.46) | collective-permute-done | bytes 524320 | tf_op jit(solution)/shard_map/ppermute | solution.py:119
  582.7 9.6 %collective-permute-done.51 = bf16[2,64,2048]{2,1,0:T(8,128)(2,1)S(1)} collective-permute-done((bf16[2,64,2048]{2,1,0:T(8,128)(2,1)S(1)}, bf16[2,64,2048]{2,1,0:T(8,128)(2,1)S(1)}, u32[]{:S(2)}, u32[]{:S(2)}) %collective-permute-start.51) | collective-permute-done | bytes 524320 | tf_op jit(solution)/shard_map/ppermute | solution.py:119
  601.8 7.1 collective-permute-done.35
  612.3 7.9 collective-permute-done.47
  623.5 7.9 collective-permute-done.52
  631.6 5.5 collective-permute-done.57
  637.2 8.4 collective-permute-done.36
  646.0 7.3 collective-permute-done.53
  654.0 6.2 collective-permute-done.58
  662.0 4.5 collective-permute-done.48
  678.0 4.3 all-to-all-start.1
  682.3 6.1 convolution_add_fusion
  699.3 7.3 all-to-all-start.6
  708.3 7.6 fusion.1
  715.9 7.9 fusion.3
  730.2 6.1 fusion.42
  737.2 11.5 %all-to-all-done.6 = bf16[16,64,512]{2,1,0:T(8,128)(2,1)S(1)} async-done(((bf16[16,64,512]{2,1,0:T(8,128)(2,1)}), bf16[16,64,512]{2,1,0:T(8,128)(2,1)S(1)}, u32[]{:S(2)}, u32[]{:S(2)}) %all-to-all-start.6) | async-done | bytes 1048608 | tf_op jit(solution)/shard_map/all_to_all | solution.py:428
  748.7 5.6 all-to-all-start.5
  754.3 9.2 %fusion.46 = bf16[1024,64]{0,1:T(8,128)(2,1)} fusion(bf16[1024,4,64]{0,2,1:T(8,128)(2,1)} %copy-done.56, f32[4,1024,1024]{1,2,0:T(8,128)} %get-tuple-element.101, f32[4,1024]{1,0:T(4,128)S(1)} %copy-done.69), kind=kOutput, calls=%fused_computation.123 | convolution fusion | flops 545325056 | bytes 17448960 | tf_op jit(solution)/shard_map/hrl,rhd->ld/dot_general | solution.py:453
  767.0 39.0 %all-to-all-done.5 = bf16[16,64,512]{2,1,0:T(8,128)(2,1)S(1)} async-done(((bf16[16,64,512]{2,1,0:T(8,128)(2,1)}), bf16[16,64,512]{2,1,0:T(8,128)(2,1)S(1)}, u32[]{:S(2)}, u32[]{:S(2)}) %all-to-all-start.5) | async-done | bytes 1048608 | tf_op jit(solution)/shard_map/all_to_all | solution.py:428
  806.0 5.4 all-to-all-start.2
  811.4 3.9 bitcast_add_fusion.2
  819.8 4.0 fusion.18
  853.0 3.6 fusion.8
  858.6 6.4 all-to-all-start.3
  867.6 4.1 collective-permute-done.69
  873.8 6.7 all-to-all-start.4
  888.8 8.4 all-to-all-done.4
  (544 shorter events, 308.3 us)
Async XLA Ops:
  7.2 306.6 %all-gather.4.cloned.1.call-start = ((), (), s32[]{:S(2)}) async-start(), calls=%async_computation.7 | async-start | bytes 8912896 | tf_op jit(solution)/shard_map/all_gather | solution.py:215
  9.2 18.8 %collective-permute-start = (bf16[64,2048]{1,0:T(8,128)(2,1)}, bf16[64,2048]{1,0:T(8,128)(2,1)}, u32[]{:S(2)}, u32[]{:S(2)}) collective-permute-start(bf16[64,2048]{1,0:T(8,128)(2,1)} %get-tuple-element.78), channel_id=1, source_target_pairs={{0,8},{1,9},{2,10},{3,11},{4,12},{5,13},{6,14},{7,15},{8,0},{9,1},... | collective-permute-start | bytes 786440 | tf_op jit(solution)/shard_map/ppermute | solution.py:116
  9.6 20.3 %collective-permute-start.2 = (bf16[64,2048]{1,0:T(8,128)(2,1)}, bf16[64,2048]{1,0:T(8,128)(2,1)}, u32[]{:S(2)}, u32[]{:S(2)}) collective-permute-start(bf16[64,2048]{1,0:T(8,128)(2,1)} %get-tuple-element.78), channel_id=1, source_target_pairs={{8,16},{9,17},{10,18},{11,19},{12,20},{13,21},{14,22},{15,23},{16,... | collective-permute-start | bytes 786440 | tf_op jit(solution)/shard_map/ppermute | solution.py:119
  26.2 138.5 %collective-permute-start.17 = (bf16[512,2048]{1,0:T(8,128)(2,1)S(1)}, bf16[512,2048]{1,0:T(8,128)(2,1)}, u32[]{:S(2)}, u32[]{:S(2)}) collective-permute-start(bf16[512,2048]{1,0:T(8,128)(2,1)S(1)} %copy-done.11), channel_id=1, source_target_pairs={{0,2},{1,3},{2,0},{3,1},{4,6},{5,7},{6,4},{7,5},{8,10},{9,11},{10,... | collective-permute-start | bytes 6291464 | tf_op jit(solution)/shard_map/ppermute | solution.py:116
  27.9 33.9 %collective-permute-start.9 = (bf16[2,64,2048]{2,1,0:T(8,128)(2,1)S(1)}, bf16[2,64,2048]{2,1,0:T(8,128)(2,1)S(1)}, u32[]{:S(2)}, u32[]{:S(2)}) collective-permute-start(bf16[2,64,2048]{2,1,0:T(8,128)(2,1)S(1)} %get-tuple-element.82), channel_id=1, source_target_pairs={{0,8},{1,9},{2,10},{3,11},{4,12},{5,13},{6,14},{7,15},{8,0},{9,1},... | collective-permute-start | bytes 1572872 | tf_op jit(solution)/shard_map/ppermute | solution.py:116
  28.0 34.4 %collective-permute-start.11 = (bf16[2,64,2048]{2,1,0:T(8,128)(2,1)S(1)}, bf16[2,64,2048]{2,1,0:T(8,128)(2,1)S(1)}, u32[]{:S(2)}, u32[]{:S(2)}) collective-permute-start(bf16[2,64,2048]{2,1,0:T(8,128)(2,1)S(1)} %get-tuple-element.82), channel_id=1, source_target_pairs={{8,16},{9,17},{10,18},{11,19},{12,20},{13,21},{14,22},{15,23},{16,... | collective-permute-start | bytes 1572872 | tf_op jit(solution)/shard_map/ppermute | solution.py:119
  29.9 30.5 %collective-permute-start.1 = (bf16[64,2048]{1,0:T(8,128)(2,1)}, bf16[64,2048]{1,0:T(8,128)(2,1)S(1)}, u32[]{:S(2)}, u32[]{:S(2)}) collective-permute-start(bf16[64,2048]{1,0:T(8,128)(2,1)} %collective-permute-done), channel_id=1, source_target_pairs={{8,16},{9,17},{10,18},{11,19},{12,20},{13,21},{14,22},{15,23},{16,... | collective-permute-start | bytes 786440 | tf_op jit(solution)/shard_map/ppermute | solution.py:119
  33.8 26.6 %collective-permute-start.3 = (bf16[64,2048]{1,0:T(8,128)(2,1)}, bf16[64,2048]{1,0:T(8,128)(2,1)S(1)}, u32[]{:S(2)}, u32[]{:S(2)}) collective-permute-start(bf16[64,2048]{1,0:T(8,128)(2,1)} %collective-permute-done.2), channel_id=1, source_target_pairs={{8,0},{9,1},{10,2},{11,3},{12,4},{13,5},{14,6},{15,7},{16,24},{17,... | collective-permute-start | bytes 786440 | tf_op jit(solution)/shard_map/ppermute | solution.py:119
  60.4 21.4 %collective-permute-start.15 = (bf16[2,512,384]{2,1,0:T(8,128)(2,1)S(1)}, bf16[2,512,384]{2,1,0:T(8,128)(2,1)S(1)}, u32[]{:S(2)}, u32[]{:S(2)}) collective-permute-start(bf16[2,512,384]{2,1,0:T(8,128)(2,1)S(1)} %pad_maximum_fusion.17), channel_id=1, source_target_pairs={{0,1},{1,0},{2,3},{3,2},{4,5},{5,4},{6,7},{7,6},{8,9},{9,8},{10,11... | collective-permute-start | bytes 2359304 | tf_op jit(solution)/shard_map/ppermute | solution.py:116
  60.4 14.9 %collective-permute-start.4 = (bf16[64,2048]{1,0:T(8,128)(2,1)S(1)}, bf16[64,2048]{1,0:T(8,128)(2,1)S(1)}, u32[]{:S(2)}, u32[]{:S(2)}) collective-permute-start(bf16[64,2048]{1,0:T(8,128)(2,1)S(1)} %collective-permute-done.1), channel_id=1, source_target_pairs={{8,0},{9,1},{10,2},{11,3},{12,4},{13,5},{14,6},{15,7},{16,24},{17,... | collective-permute-start | bytes 786440 | tf_op jit(solution)/shard_map/ppermute | solution.py:119
  61.8 114.5 %collective-permute-start.16 = (bf16[512,2048]{1,0:T(8,128)(2,1)S(1)}, bf16[512,2048]{1,0:T(8,128)(2,1)}, u32[]{:S(2)}, u32[]{:S(2)}) collective-permute-start(bf16[512,2048]{1,0:T(8,128)(2,1)S(1)} %copy-done.11), channel_id=1, source_target_pairs={{0,1},{1,0},{2,3},{3,2},{4,5},{5,4},{6,7},{7,6},{8,9},{9,8},{10,11... | collective-permute-start | bytes 6291464 | tf_op jit(solution)/shard_map/ppermute | solution.py:116
  62.4 22.5 %collective-permute-start.10 = (bf16[2,64,2048]{2,1,0:T(8,128)(2,1)S(1)}, bf16[2,64,2048]{2,1,0:T(8,128)(2,1)S(1)}, u32[]{:S(2)}, u32[]{:S(2)}) collective-permute-start(bf16[2,64,2048]{2,1,0:T(8,128)(2,1)S(1)} %collective-permute-done.9), channel_id=1, source_target_pairs={{8,16},{9,17},{10,18},{11,19},{12,20},{13,21},{14,22},{15,23},{16,... | collective-permute-start | bytes 1572872 | tf_op jit(solution)/shard_map/ppermute | solution.py:119
  75.3 25.8 %collective-permute-start.12 = (bf16[2,64,2048]{2,1,0:T(8,128)(2,1)S(1)}, bf16[2,64,2048]{2,1,0:T(8,128)(2,1)S(1)}, u32[]{:S(2)}, u32[]{:S(2)}) collective-permute-start(bf16[2,64,2048]{2,1,0:T(8,128)(2,1)S(1)} %collective-permute-done.11), channel_id=1, source_target_pairs={{8,0},{9,1},{10,2},{11,3},{12,4},{13,5},{14,6},{15,7},{16,24},{17,... | collective-permute-start | bytes 1572872 | tf_op jit(solution)/shard_map/ppermute | solution.py:119
  81.8 38.8 %collective-permute-start.5 = (bf16[4,64,2048]{2,1,0:T(8,128)(2,1)S(1)}, bf16[4,64,2048]{2,1,0:T(8,128)(2,1)S(1)}, u32[]{:S(2)}, u32[]{:S(2)}) collective-permute-start(bf16[4,64,2048]{2,1,0:T(8,128)(2,1)S(1)} %get-tuple-element.66), channel_id=1, source_target_pairs={{0,4},{1,5},{2,6},{3,7},{4,0},{5,1},{6,2},{7,3},{8,12},{9,13},{10,... | collective-permute-start | bytes 3145736 | tf_op jit(solution)/shard_map/ppermute | solution.py:116
  84.9 32.8 %collective-permute-start.13 = (bf16[2,64,2048]{2,1,0:T(8,128)(2,1)S(1)}, bf16[2,64,2048]{2,1,0:T(8,128)(2,1)S(1)}, u32[]{:S(2)}, u32[]{:S(2)}) collective-permute-start(bf16[2,64,2048]{2,1,0:T(8,128)(2,1)S(1)} %collective-permute-done.10), channel_id=1, source_target_pairs={{8,0},{9,1},{10,2},{11,3},{12,4},{13,5},{14,6},{15,7},{16,24},{17,... | collective-permute-start | bytes 1572872 | tf_op jit(solution)/shard_map/ppermute | solution.py:119
  155.0 18.1 %all-to-all-start = ((bf16[8,128,256]{2,1,0:T(8,128)(2,1)}), bf16[8,128,256]{2,1,0:T(8,128)(2,1)S(1)}, u32[]{:S(2)}, u32[]{:S(2)}) async-start(bf16[8,128,256]{2,1,0:T(8,128)(2,1)} %bitcast.44), calls=%async_computation | async-start | bytes 1048576 | tf_op jit(solution)/shard_map/all_to_all | solution.py:353
  164.7 13.6 %collective-permute-start.18 = (bf16[512,2048]{1,0:T(8,128)(2,1)}, bf16[512,2048]{1,0:T(8,128)(2,1)}, u32[]{:S(2)}, u32[]{:S(2)}) collective-permute-start(bf16[512,2048]{1,0:T(8,128)(2,1)} %collective-permute-done.17), channel_id=1, source_target_pairs={{0,1},{1,0},{2,3},{3,2},{4,5},{5,4},{6,7},{7,6},{8,9},{9,8},{10,11... | collective-permute-start | bytes 6291464 | tf_op jit(solution)/shard_map/ppermute | solution.py:116
  166.7 24.0 %collective-permute-start.26 = (bf16[512,512]{1,0:T(8,128)(2,1)}, bf16[512,512]{1,0:T(8,128)(2,1)}, u32[]{:S(2)}, u32[]{:S(2)}) collective-permute-start(bf16[512,512]{1,0:T(8,128)(2,1)} %constant_dynamic-slice_fusion.2), channel_id=1, source_target_pairs={{0,2},{1,3},{2,0},{3,1},{4,6},{5,7},{6,4},{7,5},{8,10},{9,11},{10,... | collective-permute-start | bytes 1572872 | tf_op jit(solution)/shard_map/ppermute | solution.py:116
  168.6 24.5 %collective-permute-start.28 = (bf16[512,512]{1,0:T(8,128)(2,1)}, bf16[512,512]{1,0:T(8,128)(2,1)}, u32[]{:S(2)}, u32[]{:S(2)}) collective-permute-start(bf16[512,512]{1,0:T(8,128)(2,1)} %constant_dynamic-slice_fusion.1), channel_id=1, source_target_pairs={{0,2},{1,3},{2,0},{3,1},{4,6},{5,7},{6,4},{7,5},{8,10},{9,11},{10,... | collective-permute-start | bytes 1572872 | tf_op jit(solution)/shard_map/ppermute | solution.py:116
  184.4 14.5 %collective-permute-start.21 = (bf16[64,2048]{1,0:T(8,128)(2,1)S(1)}, bf16[64,2048]{1,0:T(8,128)(2,1)}, u32[]{:S(2)}, u32[]{:S(2)}) collective-permute-start(bf16[64,2048]{1,0:T(8,128)(2,1)S(1)} %get-tuple-element.76), channel_id=1, source_target_pairs={{8,16},{9,17},{10,18},{11,19},{12,20},{13,21},{14,22},{15,23},{16,... | collective-permute-start | bytes 786440 | tf_op jit(solution)/shard_map/ppermute | solution.py:119
  188.6 36.0 %collective-permute-start.30 = (bf16[512,2048]{1,0:T(8,128)(2,1)S(1)}, bf16[512,2048]{1,0:T(8,128)(2,1)}, u32[]{:S(2)}, u32[]{:S(2)}) collective-permute-start(bf16[512,2048]{1,0:T(8,128)(2,1)S(1)} %constant_dynamic-slice_fusion), channel_id=1, source_target_pairs={{0,2},{4,6},{9,11},{13,15},{18,16},{22,20},{27,25},{31,29}} | collective-permute-start | bytes 6291464 | tf_op jit(solution)/shard_map/ppermute | solution.py:119
  196.0 14.0 %collective-permute-start.20 = (bf16[64,2048]{1,0:T(8,128)(2,1)}, bf16[64,2048]{1,0:T(8,128)(2,1)S(1)}, u32[]{:S(2)}, u32[]{:S(2)}) collective-permute-start(bf16[64,2048]{1,0:T(8,128)(2,1)} %collective-permute-done.19), channel_id=1, source_target_pairs={{8,16},{9,17},{10,18},{11,19},{12,20},{13,21},{14,22},{15,23},{16,... | collective-permute-start | bytes 786440 | tf_op jit(solution)/shard_map/ppermute | solution.py:119
  221.0 21.4 %collective-permute-start.24 = (bf16[4,64,2048]{2,1,0:T(8,128)(2,1)S(1)}, bf16[4,64,2048]{2,1,0:T(8,128)(2,1)S(1)}, u32[]{:S(2)}, u32[]{:S(2)}) collective-permute-start(bf16[4,64,2048]{2,1,0:T(8,128)(2,1)S(1)} %get-tuple-element.62), channel_id=1, source_target_pairs={{0,4},{1,5},{2,6},{3,7},{4,0},{5,1},{6,2},{7,3},{8,12},{9,13},{10,... | collective-permute-start | bytes 3145736 | tf_op jit(solution)/shard_map/ppermute | solution.py:116
  224.1 26.3 %collective-permute-start.42 = (bf16[4,64,2048]{2,1,0:T(8,128)(2,1)}, bf16[4,64,2048]{2,1,0:T(8,128)(2,1)}, u32[]{:S(2)}, u32[]{:S(2)}) collective-permute-start(bf16[4,64,2048]{2,1,0:T(8,128)(2,1)} %get-tuple-element.64), channel_id=1, source_target_pairs={{0,2},{1,3},{2,0},{3,1},{4,6},{5,7},{6,4},{7,5},{8,10},{9,11},{10,... | collective-permute-start | bytes 3145736 | tf_op jit(solution)/shard_map/ppermute | solution.py:116
  227.7 37.0 %collective-permute-start.31 = (bf16[512,2048]{1,0:T(8,128)(2,1)S(1)}, bf16[512,2048]{1,0:T(8,128)(2,1)}, u32[]{:S(2)}, u32[]{:S(2)}) collective-permute-start(bf16[512,2048]{1,0:T(8,128)(2,1)S(1)} %dynamic-slice_select_fusion), channel_id=1, source_target_pairs={{0,1},{1,0},{2,3},{3,2},{4,5},{5,4},{6,7},{7,6},{8,9},{9,8},{10,11... | collective-permute-start | bytes 6291464 | tf_op jit(solution)/shard_map/ppermute | solution.py:116
  228.8 27.2 %collective-permute-start.29 = (bf16[2,512,512]{2,1,0:T(8,128)(2,1)}, bf16[2,512,512]{2,1,0:T(8,128)(2,1)}, u32[]{:S(2)}, u32[]{:S(2)}) collective-permute-start(bf16[2,512,512]{2,1,0:T(8,128)(2,1)} %pad_maximum_fusion.13), channel_id=1, source_target_pairs={{0,1},{1,0},{2,3},{3,2},{4,5},{5,4},{6,7},{7,6},{8,9},{9,8},{10,11... | collective-permute-start | bytes 3145736 | tf_op jit(solution)/shard_map/ppermute | solution.py:116
  230.4 28.9 %collective-permute-start.27 = (bf16[2,512,512]{2,1,0:T(8,128)(2,1)}, bf16[2,512,512]{2,1,0:T(8,128)(2,1)}, u32[]{:S(2)}, u32[]{:S(2)}) collective-permute-start(bf16[2,512,512]{2,1,0:T(8,128)(2,1)} %pad_maximum_fusion.12), channel_id=1, source_target_pairs={{0,1},{1,0},{2,3},{3,2},{4,5},{5,4},{6,7},{7,6},{8,9},{9,8},{10,11... | collective-permute-start | bytes 3145736 | tf_op jit(solution)/shard_map/ppermute | solution.py:116
  244.7 48.0 %collective-permute-start.25 = (bf16[2,4,64,2048]{3,2,1,0:T(8,128)(2,1)}, bf16[2,4,64,2048]{3,2,1,0:T(8,128)(2,1)}, u32[]{:S(2)}, u32[]{:S(2)}) collective-permute-start(bf16[2,4,64,2048]{3,2,1,0:T(8,128)(2,1)} %get-tuple-element.47), channel_id=1, source_target_pairs={{0,2},{1,3},{2,0},{3,1},{4,6},{5,7},{6,4},{7,5},{8,10},{9,11},{10,... | collective-permute-start | bytes 6291464 | tf_op jit(solution)/shard_map/ppermute | solution.py:116
  254.3 42.4 %collective-permute-start.43 = (bf16[2,4,64,2048]{3,2,1,0:T(8,128)(2,1)}, bf16[2,4,64,2048]{3,2,1,0:T(8,128)(2,1)}, u32[]{:S(2)}, u32[]{:S(2)}) collective-permute-start(bf16[2,4,64,2048]{3,2,1,0:T(8,128)(2,1)} %get-tuple-element.53), channel_id=1, source_target_pairs={{0,4},{1,5},{2,6},{3,7},{4,0},{5,1},{6,2},{7,3},{8,12},{9,13},{10,... | collective-permute-start | bytes 6291464 | tf_op jit(solution)/shard_map/ppermute | solution.py:116
  256.0 573.1 %collective-permute-start.60 = (bf16[512,512]{1,0:T(8,128)(2,1)}, bf16[512,512]{1,0:T(8,128)(2,1)}, u32[]{:S(2)}, u32[]{:S(2)}) collective-permute-start(bf16[512,512]{1,0:T(8,128)(2,1)} %param.19), channel_id=1, source_target_pairs={{0,1},{1,0},{2,3},{3,2},{4,5},{5,4},{6,7},{7,6},{8,9},{9,8},{10,11... | collective-permute-start | bytes 1572872 | tf_op jit(solution)/shard_map/ppermute | solution.py:116
  259.3 576.1 %collective-permute-start.61 = (bf16[512,512]{1,0:T(8,128)(2,1)}, bf16[512,512]{1,0:T(8,128)(2,1)}, u32[]{:S(2)}, u32[]{:S(2)}) collective-permute-start(bf16[512,512]{1,0:T(8,128)(2,1)} %param.20), channel_id=1, source_target_pairs={{0,1},{1,0},{2,3},{3,2},{4,5},{5,4},{6,7},{7,6},{8,9},{9,8},{10,11... | collective-permute-start | bytes 1572872 | tf_op jit(solution)/shard_map/ppermute | solution.py:116
  414.0 48.8 %collective-permute-start.32 = (bf16[2,4,64,2048]{3,2,1,0:T(8,128)(2,1)}, bf16[2,4,64,2048]{3,2,1,0:T(8,128)(2,1)}, u32[]{:S(2)}, u32[]{:S(2)}) collective-permute-start(bf16[2,4,64,2048]{3,2,1,0:T(8,128)(2,1)} %bitcast.70), channel_id=1, source_target_pairs={{0,2},{1,3},{2,0},{3,1},{4,6},{5,7},{6,4},{7,5},{8,10},{9,11},{10,... | collective-permute-start | bytes 6291464 | tf_op jit(solution)/shard_map/ppermute | solution.py:116
  419.4 48.7 %collective-permute-start.44 = (bf16[2,4,64,2048]{3,2,1,0:T(8,128)(2,1)}, bf16[2,4,64,2048]{3,2,1,0:T(8,128)(2,1)S(1)}, u32[]{:S(2)}, u32[]{:S(2)}) collective-permute-start(bf16[2,4,64,2048]{3,2,1,0:T(8,128)(2,1)} %bitcast.85), channel_id=1, source_target_pairs={{0,4},{1,5},{2,6},{3,7},{4,0},{5,1},{6,2},{7,3},{8,12},{9,13},{10,... | collective-permute-start | bytes 6291464 | tf_op jit(solution)/shard_map/ppermute | solution.py:116
  432.3 75.4 %collective-permute-start.49 = (bf16[2,4,64,2048]{3,2,1,0:T(8,128)(2,1)}, bf16[2,4,64,2048]{3,2,1,0:T(8,128)(2,1)}, u32[]{:S(2)}, u32[]{:S(2)}) collective-permute-start(bf16[2,4,64,2048]{3,2,1,0:T(8,128)(2,1)} %bitcast.97), channel_id=1, source_target_pairs={{0,2},{1,3},{2,0},{3,1},{4,6},{5,7},{6,4},{7,5},{8,10},{9,11},{10,... | collective-permute-start | bytes 6291464 | tf_op jit(solution)/shard_map/ppermute | solution.py:116
  462.8 50.2 %collective-permute-start.54 = (bf16[2,4,64,2048]{3,2,1,0:T(8,128)(2,1)S(1)}, bf16[2,4,64,2048]{3,2,1,0:T(8,128)(2,1)S(1)}, u32[]{:S(2)}, u32[]{:S(2)}) collective-permute-start(bf16[2,4,64,2048]{3,2,1,0:T(8,128)(2,1)S(1)} %bitcast.535), channel_id=1, source_target_pairs={{0,4},{1,5},{2,6},{3,7},{4,0},{5,1},{6,2},{7,3},{8,12},{9,13},{10,... | collective-permute-start | bytes 6291464 | tf_op jit(solution)/shard_map/ppermute | solution.py:116
  468.1 359.6 %collective-permute-start.63 = (bf16[512,512]{1,0:T(8,128)(2,1)}, bf16[512,512]{1,0:T(8,128)(2,1)}, u32[]{:S(2)}, u32[]{:S(2)}) collective-permute-start(bf16[512,512]{1,0:T(8,128)(2,1)} %param.19), channel_id=1, source_target_pairs={{0,2},{1,3},{2,0},{3,1},{4,6},{5,7},{6,4},{7,5},{8,10},{9,11},{10,... | collective-permute-start | bytes 1572872 | tf_op jit(solution)/shard_map/ppermute | solution.py:116
  507.7 25.1 %collective-permute-start.33 = (bf16[4,64,2048]{2,1,0:T(8,128)(2,1)S(1)}, bf16[4,64,2048]{2,1,0:T(8,128)(2,1)S(1)}, u32[]{:S(2)}, u32[]{:S(2)}) collective-permute-start(bf16[4,64,2048]{2,1,0:T(8,128)(2,1)S(1)} %fusion.49), channel_id=1, source_target_pairs={{0,4},{1,5},{2,6},{3,7},{4,0},{5,1},{6,2},{7,3},{8,12},{9,13},{10,... | collective-permute-start | bytes 3145736 | tf_op jit(solution)/shard_map/ppermute | solution.py:116
  513.0 25.6 %collective-permute-start.45 = (bf16[4,64,2048]{2,1,0:T(8,128)(2,1)S(1)}, bf16[4,64,2048]{2,1,0:T(8,128)(2,1)S(1)}, u32[]{:S(2)}, u32[]{:S(2)}) collective-permute-start(bf16[4,64,2048]{2,1,0:T(8,128)(2,1)S(1)} %fusion.50), channel_id=1, source_target_pairs={{0,2},{1,3},{2,0},{3,1},{4,6},{5,7},{6,4},{7,5},{8,10},{9,11},{10,... | collective-permute-start | bytes 3145736 | tf_op jit(solution)/shard_map/ppermute | solution.py:116
  532.8 20.8 %collective-permute-start.50 = (bf16[4,64,2048]{2,1,0:T(8,128)(2,1)S(1)}, bf16[4,64,2048]{2,1,0:T(8,128)(2,1)S(1)}, u32[]{:S(2)}, u32[]{:S(2)}) collective-permute-start(bf16[4,64,2048]{2,1,0:T(8,128)(2,1)S(1)} %fusion.51), channel_id=1, source_target_pairs={{0,4},{1,5},{2,6},{3,7},{4,0},{5,1},{6,2},{7,3},{8,12},{9,13},{10,... | collective-permute-start | bytes 3145736 | tf_op jit(solution)/shard_map/ppermute | solution.py:116
  538.6 21.1 %collective-permute-start.55 = (bf16[4,64,2048]{2,1,0:T(8,128)(2,1)S(1)}, bf16[4,64,2048]{2,1,0:T(8,128)(2,1)S(1)}, u32[]{:S(2)}, u32[]{:S(2)}) collective-permute-start(bf16[4,64,2048]{2,1,0:T(8,128)(2,1)S(1)} %fusion.52), channel_id=1, source_target_pairs={{0,2},{1,3},{2,0},{3,1},{4,6},{5,7},{6,4},{7,5},{8,10},{9,11},{10,... | collective-permute-start | bytes 3145736 | tf_op jit(solution)/shard_map/ppermute | solution.py:116
  553.6 16.2 %collective-permute-start.34 = (bf16[2,64,2048]{2,1,0:T(8,128)(2,1)S(1)}, bf16[2,64,2048]{2,1,0:T(8,128)(2,1)S(1)}, u32[]{:S(2)}, u32[]{:S(2)}) collective-permute-start(bf16[2,64,2048]{2,1,0:T(8,128)(2,1)S(1)} %stack.321), channel_id=1, source_target_pairs={{0,8},{1,9},{2,10},{3,11},{4,12},{5,13},{6,14},{7,15},{24,16},{25,... | collective-permute-start | bytes 1572872 | tf_op jit(solution)/shard_map/ppermute | solution.py:119
  559.7 21.4 %collective-permute-start.46 = (bf16[2,64,2048]{2,1,0:T(8,128)(2,1)S(1)}, bf16[2,64,2048]{2,1,0:T(8,128)(2,1)S(1)}, u32[]{:S(2)}, u32[]{:S(2)}) collective-permute-start(bf16[2,64,2048]{2,1,0:T(8,128)(2,1)S(1)} %stack.320), channel_id=1, source_target_pairs={{0,8},{1,9},{2,10},{3,11},{4,12},{5,13},{6,14},{7,15},{24,16},{25,... | collective-permute-start | bytes 1572872 | tf_op jit(solution)/shard_map/ppermute | solution.py:119
  569.8 22.5 %collective-permute-start.51 = (bf16[2,64,2048]{2,1,0:T(8,128)(2,1)S(1)}, bf16[2,64,2048]{2,1,0:T(8,128)(2,1)S(1)}, u32[]{:S(2)}, u32[]{:S(2)}) collective-permute-start(bf16[2,64,2048]{2,1,0:T(8,128)(2,1)S(1)} %stack.319), channel_id=1, source_target_pairs={{0,8},{1,9},{2,10},{3,11},{4,12},{5,13},{6,14},{7,15},{24,16},{25,... | collective-permute-start | bytes 1572872 | tf_op jit(solution)/shard_map/ppermute | solution.py:119
  581.0 17.3 %collective-permute-start.56 = (bf16[2,64,2048]{2,1,0:T(8,128)(2,1)S(1)}, bf16[2,64,2048]{2,1,0:T(8,128)(2,1)S(1)}, u32[]{:S(2)}, u32[]{:S(2)}) collective-permute-start(bf16[2,64,2048]{2,1,0:T(8,128)(2,1)S(1)} %stack.318), channel_id=1, source_target_pairs={{0,8},{1,9},{2,10},{3,11},{4,12},{5,13},{6,14},{7,15},{24,16},{25,... | collective-permute-start | bytes 1572872 | tf_op jit(solution)/shard_map/ppermute | solution.py:119
  592.3 16.7 %collective-permute-start.35 = (bf16[2,64,2048]{2,1,0:T(8,128)(2,1)S(1)}, bf16[2,64,2048]{2,1,0:T(8,128)(2,1)S(1)}, u32[]{:S(2)}, u32[]{:S(2)}) collective-permute-start(bf16[2,64,2048]{2,1,0:T(8,128)(2,1)S(1)} %pad_maximum_fusion.21), channel_id=1, source_target_pairs={{8,16},{9,17},{10,18},{11,19},{12,20},{13,21},{14,22},{15,23},{16,... | collective-permute-start | bytes 1572872 | tf_op jit(solution)/shard_map/ppermute | solution.py:119
  598.3 21.9 %collective-permute-start.47 = (bf16[2,64,2048]{2,1,0:T(8,128)(2,1)S(1)}, bf16[2,64,2048]{2,1,0:T(8,128)(2,1)S(1)}, u32[]{:S(2)}, u32[]{:S(2)}) collective-permute-start(bf16[2,64,2048]{2,1,0:T(8,128)(2,1)S(1)} %pad_maximum_fusion.22), channel_id=1, source_target_pairs={{8,16},{9,17},{10,18},{11,19},{12,20},{13,21},{14,22},{15,23},{16,... | collective-permute-start | bytes 1572872 | tf_op jit(solution)/shard_map/ppermute | solution.py:119
  609.0 22.5 %collective-permute-start.52 = (bf16[2,64,2048]{2,1,0:T(8,128)(2,1)S(1)}, bf16[2,64,2048]{2,1,0:T(8,128)(2,1)S(1)}, u32[]{:S(2)}, u32[]{:S(2)}) collective-permute-start(bf16[2,64,2048]{2,1,0:T(8,128)(2,1)S(1)} %pad_maximum_fusion.23), channel_id=1, source_target_pairs={{8,16},{9,17},{10,18},{11,19},{12,20},{13,21},{14,22},{15,23},{16,... | collective-permute-start | bytes 1572872 | tf_op jit(solution)/shard_map/ppermute | solution.py:119
  620.2 16.9 %collective-permute-start.57 = (bf16[2,64,2048]{2,1,0:T(8,128)(2,1)S(1)}, bf16[2,64,2048]{2,1,0:T(8,128)(2,1)S(1)}, u32[]{:S(2)}, u32[]{:S(2)}) collective-permute-start(bf16[2,64,2048]{2,1,0:T(8,128)(2,1)S(1)} %pad_maximum_fusion.24), channel_id=1, source_target_pairs={{8,16},{9,17},{10,18},{11,19},{12,20},{13,21},{14,22},{15,23},{16,... | collective-permute-start | bytes 1572872 | tf_op jit(solution)/shard_map/ppermute | solution.py:119
  631.4 60.1 %collective-permute-start.73 = (f32[16,64,512]{2,1,0:T(8,128)}, f32[16,64,512]{2,1,0:T(8,128)}, u32[]{:S(2)}, u32[]{:S(2)}) collective-permute-start(f32[16,64,512]{2,1,0:T(8,128)} %dynamic-slice_bitcast_fusion.1), channel_id=1, source_target_pairs={{0,1},{1,0},{2,3},{3,2},{4,5},{5,4},{6,7},{7,6},{8,9},{9,8},{10,11... | collective-permute-start | bytes 6291464 | tf_op jit(solution)/shard_map/ppermute | solution.py:116
  666.5 29.8 %collective-permute-start.72 = (f32[16,64,512]{2,1,0:T(8,128)}, f32[16,64,512]{2,1,0:T(8,128)}, u32[]{:S(2)}, u32[]{:S(2)}) collective-permute-start(f32[16,64,512]{2,1,0:T(8,128)} %dynamic-slice_bitcast_fusion.2), channel_id=1, source_target_pairs={{0,1},{1,0},{2,3},{3,2},{4,5},{5,4},{6,7},{7,6},{8,9},{9,8},{10,11... | collective-permute-start | bytes 6291464 | tf_op jit(solution)/shard_map/ppermute | solution.py:116
  678.0 21.3 %all-to-all-start.1 = ((bf16[128,8,256]{0,2,1:T(8,128)(2,1)}), bf16[128,8,256]{0,2,1:T(8,128)(2,1)S(1)}, u32[]{:S(2)}, u32[]{:S(2)}) async-start(bf16[128,8,256]{0,2,1:T(8,128)(2,1)} %bitcast.111), calls=%async_computation.1 | async-start | bytes 1048576 | tf_op jit(solution)/shard_map/all_to_all | solution.py:438
  682.3 170.7 %all-gather.6.cloned.1.call-start = ((), (), s32[]{:S(2)}) async-start(), calls=%async_computation.8 | async-start | bytes 4718592 | tf_op jit(solution)/shard_map/all_gather | solution.py:153
  691.6 138.2 %collective-permute-start.64 = (bf16[512,512]{1,0:T(8,128)(2,1)}, bf16[512,512]{1,0:T(8,128)(2,1)}, u32[]{:S(2)}, u32[]{:S(2)}) collective-permute-start(bf16[512,512]{1,0:T(8,128)(2,1)} %param.20), channel_id=1, source_target_pairs={{0,2},{1,3},{2,0},{3,1},{4,6},{5,7},{6,4},{7,5},{8,10},{9,11},{10,... | collective-permute-start | bytes 1572872 | tf_op jit(solution)/shard_map/ppermute | solution.py:116
  696.3 70.1 %collective-permute-start.74 = (f32[256,2048]{1,0:T(8,128)}, f32[256,2048]{1,0:T(8,128)}, u32[]{:S(2)}, u32[]{:S(2)}) collective-permute-start(f32[256,2048]{1,0:T(8,128)} %dynamic-slice_bitcast_fusion), channel_id=1, source_target_pairs={{0,1},{1,0},{2,3},{3,2},{4,5},{5,4},{6,7},{7,6},{8,9},{9,8},{10,11... | collective-permute-start | bytes 6291464 | tf_op jit(solution)/shard_map/ppermute | solution.py:116
  699.3 49.4 %all-to-all-start.6 = ((bf16[16,64,512]{2,1,0:T(8,128)(2,1)}), bf16[16,64,512]{2,1,0:T(8,128)(2,1)S(1)}, u32[]{:S(2)}, u32[]{:S(2)}) async-start(bf16[16,64,512]{2,1,0:T(8,128)(2,1)} %fusion.25), calls=%async_computation.6 | async-start | bytes 2097152 | tf_op jit(solution)/shard_map/all_to_all | solution.py:428
  748.7 57.3 %all-to-all-start.5 = ((bf16[16,64,512]{2,1,0:T(8,128)(2,1)}), bf16[16,64,512]{2,1,0:T(8,128)(2,1)S(1)}, u32[]{:S(2)}, u32[]{:S(2)}) async-start(bf16[16,64,512]{2,1,0:T(8,128)(2,1)} %fusion.26), calls=%async_computation.5 | async-start | bytes 2097152 | tf_op jit(solution)/shard_map/all_to_all | solution.py:428
  766.4 63.4 %collective-permute-start.62 = (bf16[512,2048]{1,0:T(8,128)(2,1)}, bf16[512,2048]{1,0:T(8,128)(2,1)}, u32[]{:S(2)}, u32[]{:S(2)}) collective-permute-start(bf16[512,2048]{1,0:T(8,128)(2,1)} %param.18), channel_id=1, source_target_pairs={{0,2},{1,3},{2,0},{3,1},{4,6},{5,7},{6,4},{7,5},{8,10},{9,11},{10,... | collective-permute-start | bytes 6291464 | tf_op jit(solution)/shard_map/ppermute | solution.py:116
  806.0 21.0 %all-to-all-start.2 = ((bf16[8,128,384]{2,1,0:T(8,128)(2,1)}), bf16[8,128,384]{2,1,0:T(8,128)(2,1)S(1)}, u32[]{:S(2)}, u32[]{:S(2)}) async-start(bf16[8,128,384]{2,1,0:T(8,128)(2,1)} %bitcast.513), calls=%async_computation.2 | async-start | bytes 1572864 | tf_op jit(solution)/shard_map/all_to_all | solution.py:485
  827.7 15.0 %collective-permute-start.59 = (bf16[512,2048]{1,0:T(8,128)(2,1)}, bf16[512,2048]{1,0:T(8,128)(2,1)S(1)}, u32[]{:S(2)}, u32[]{:S(2)}) collective-permute-start(bf16[512,2048]{1,0:T(8,128)(2,1)} %param.18), channel_id=1, source_target_pairs={{0,1},{1,0},{2,3},{3,2},{4,5},{5,4},{6,7},{7,6},{8,9},{9,8},{10,11... | collective-permute-start | bytes 6291464 | tf_op jit(solution)/shard_map/ppermute | solution.py:116
  829.8 13.7 %collective-permute-start.65 = (bf16[512,2048]{1,0:T(8,128)(2,1)}, bf16[512,2048]{1,0:T(8,128)(2,1)S(1)}, u32[]{:S(2)}, u32[]{:S(2)}) collective-permute-start(bf16[512,2048]{1,0:T(8,128)(2,1)} %collective-permute-done.62), channel_id=1, source_target_pairs={{0,1},{1,0},{2,3},{3,2},{4,5},{5,4},{6,7},{7,6},{8,9},{9,8},{10,11... | collective-permute-start | bytes 6291464 | tf_op jit(solution)/shard_map/ppermute | solution.py:116
  851.5 20.2 %collective-permute-start.69 = (f32[8,64,384]{2,1,0:T(8,128)}, f32[8,64,384]{2,1,0:T(8,128)S(1)}, u32[]{:S(2)}, u32[]{:S(2)}) collective-permute-start(f32[8,64,384]{2,1,0:T(8,128)} %dynamic-slice_bitcast_fusion.5), channel_id=1, source_target_pairs={{0,2},{1,3},{2,0},{3,1},{4,6},{5,7},{6,4},{7,5},{8,10},{9,11},{10,... | collective-permute-start | bytes 2359304 | tf_op jit(solution)/shard_map/ppermute | solution.py:116
  857.7 26.9 %collective-permute-start.70 = (f32[2,64,2048]{2,1,0:T(8,128)}, f32[2,64,2048]{2,1,0:T(8,128)}, u32[]{:S(2)}, u32[]{:S(2)}) collective-permute-start(f32[2,64,2048]{2,1,0:T(8,128)} %dynamic-slice_bitcast_fusion.4), channel_id=1, source_target_pairs={{0,1},{1,0},{2,3},{3,2},{4,5},{5,4},{6,7},{7,6},{8,9},{9,8},{10,11... | collective-permute-start | bytes 3145736 | tf_op jit(solution)/shard_map/ppermute | solution.py:116
  858.6 15.3 %all-to-all-start.3 = ((f32[32,1,128]{2,1,0:T(1,128)}), f32[32,1,128]{2,1,0:T(1,128)S(1)}, u32[]{:S(2)}, u32[]{:S(2)}) async-start(f32[32,1,128]{2,1,0:T(1,128)} %reshape.591), calls=%async_computation.3 | async-start | bytes 32768 | tf_op jit(solution)/shard_map/all_to_all | solution.py:509
  873.8 23.4 %all-to-all-start.4 = ((f32[8,64,384]{2,1,0:T(8,128)}), f32[8,64,384]{2,1,0:T(8,128)S(1)}, u32[]{:S(2)}, u32[]{:S(2)}) async-start(f32[8,64,384]{2,1,0:T(8,128)} %bitcast_add_fusion.5), calls=%async_computation.4 | async-start | bytes 1572864 | tf_op jit(solution)/shard_map/all_to_all | solution.py:503
  (104 other events, 1468.7 us)
Sparse Core Ops, SparseCore 0:
  22.3 136.3 all-gather.3
  699.4 110.1 all-gather.5
where the time goes:
time: 920 us; the launch traced here: 908 us
  waiting for transfers between devices  370 us (40%)
  matrix products  156 us (17%)
  other arithmetic  151 us (16%)
  starting transfers between devices  132 us (14%)
  local copies, waits for them, and re-layouts  83.4 us (9%)
  between operations  16.9 us (2%)
    ppermute x50, waiting for transfers between devices, swap(): lax.ppermute(value, EVERY, [(i, i ^ bits) for i in range(self.total)])  173 us
    ppermute x25, waiting for transfers between devices, send(): return lax.ppermute(value, EVERY, pairs)  135 us
    select_n x4, other arithmetic, spread_late(): held = jnp.where(bit == 1, jnp.flip(held, step), held)  58.7 us
    ppermute x25, starting transfers between devices, send(): return lax.ppermute(value, EVERY, pairs)  57.4 us
    dot_general x22, matrix products, mm_t(): return jnp.einsum('ij,kj->ik', left, right, preferred_element_type=wide)  54.6 us
    all_to_all x2, waiting for transfers between devices, columns_out(): moved = lax.all_to_all(parts.astype(low), CHIPS, 0, 0, tiled=True)  50.6 us
    dot_general x8, matrix products, t_mm(): return jnp.einsum('ti,tj->ij', left, right, preferred_element_type=wide)  30.3 us
    ppermute x50, starting transfers between devices, swap(): lax.ppermute(value, EVERY, [(i, i ^ bits) for i in range(self.total)])  29.1 us
  transfers between devices with their start and end apart: 84, of which 40 were waited for; matrix products, arithmetic and copies ran while one was open for 41% of the time, Pallas kernels for 0%

commit v1 on v0

--- a/solution.py
+++ b/solution.py
@@ -212,15 +212,15 @@
             return self.spread(value)
         half = value.shape[0] // 2
         width = value.shape[1]
-        held = lax.all_gather(value, CHIPS, axis=0, tiled=False)
-        held = held.reshape(2, 2, 2, 2, 2, half, width)
-        bits = ((self.c >> 2) & 1, (self.c >> 1) & 1, self.c & 1, self.x)
-        for step, bit in enumerate(bits):
-            held = jnp.where(bit == 1, jnp.flip(held, step), held)
-        return [
-            held[:, :, :, :, part].transpose(order).reshape(16 * half, width)
-            for part, order in enumerate(((3, 2, 0, 1, 4, 5), (2, 3, 0, 1, 4, 5)))
-        ]
+        found = []
+        for rows, order in ((value[:half], (3, 2, 0, 1, 4, 5)), (value[half:], (2, 3, 0, 1, 4, 5))):
+            held = lax.all_gather(rows, CHIPS, axis=0, tiled=False)
+            held = held.reshape(2, 2, 2, 2, half, width)
+            bits = ((self.c >> 2) & 1, (self.c >> 1) & 1, self.c & 1, self.x)
+            for step, bit in enumerate(bits):
+                held = jnp.where(bit == 1, jnp.flip(held, step), held)
+            found.append(held.transpose(order).reshape(16 * half, width))
+        return found
 
     def collect(self, parts):
         if not self.paths:

time: 920 us -> 944 us (1.026)
  waiting for transfers between devices: 370 us -> 444 us
  other arithmetic: 151 us -> 111 us
    ppermute x50, waiting for transfers between devices: 173 us -> 251 us  [swap(): lax.ppermute(value, EVERY, [(i, i ^ bits) for i in range(self.total)])]
    select_n x4 -> x5, other arithmetic: 58.7 us -> 13.8 us  [spread_late(): held = jnp.where(bit == 1, jnp.flip(held, step), held)]
  transfers between devices with their start and end apart: 84 -> 85, of which waited for: 40 -> 42; matrix products, arithmetic and copies ran while one was open for 41% -> 36% of each run, Pallas kernels for 0% -> 0%
where the time goes in v1:
time: 944 us; the launch traced here: 931 us
  waiting for transfers between devices  444 us (47%)
  matrix products  154 us (16%)
  starting transfers between devices  124 us (13%)
  other arithmetic  111 us (12%)
  local copies, waits for them, and re-layouts  80.9 us (9%)
  between operations  16.5 us (2%)
    ppermute x50, waiting for transfers between devices, swap(): lax.ppermute(value, EVERY, [(i, i ^ bits) for i in range(self.total)])  251 us
    ppermute x25, waiting for transfers between devices, send(): return lax.ppermute(value, EVERY, pairs)  128 us
    dot_general x22, matrix products, mm_t(): return jnp.einsum('ij,kj->ik', left, right, preferred_element_type=wide)  56 us
    ppermute x25, starting transfers between devices, send(): return lax.ppermute(value, EVERY, pairs)  54.4 us
    all_to_all x2, waiting for transfers between devices, columns_out(): moved = lax.all_to_all(parts.astype(low), CHIPS, 0, 0, tiled=True)  50.6 us
    dot_general x8, matrix products, t_mm(): return jnp.einsum('ti,tj->ij', left, right, preferred_element_type=wide)  30.1 us
    ppermute x50, starting transfers between devices, swap(): lax.ppermute(value, EVERY, [(i, i ^ bits) for i in range(self.total)])  26.6 us
    dot_general x11, matrix products, mm(): return jnp.dot(left, right, preferred_element_type=wide)  24.3 us
  transfers between devices with their start and end apart: 85, of which 42 were waited for; matrix products, arithmetic and copies ran while one was open for 36% of the time, Pallas kernels for 0%

profile of v1, /device:TPU:14, one launch (start us, length us, event | category | flops | bytes accessed | tf_op | source)
XLA Modules:
  0.0 930.7 jit_solution(14538666926693530031)
XLA Ops:
  11.7 4.6 collective-permute-start.2
  43.7 10.3 %collective-permute-done.1 = bf16[64,2048]{1,0:T(8,128)(2,1)S(1)} collective-permute-done((bf16[64,2048]{1,0:T(8,128)(2,1)}, bf16[64,2048]{1,0:T(8,128)(2,1)S(1)}, u32[]{:S(2)}, u32[]{:S(2)}) %collective-permute-start.1) | collective-permute-done | bytes 262176 | tf_op jit(solution)/shard_map/ppermute | solution.py:119
  56.5 60.4 %collective-permute-done.26 = bf16[512,512]{1,0:T(8,128)(2,1)S(1)} collective-permute-done((bf16[512,512]{1,0:T(8,128)(2,1)}, bf16[512,512]{1,0:T(8,128)(2,1)S(1)}, u32[]{:S(2)}, u32[]{:S(2)}) %collective-permute-start.26) | collective-permute-done | bytes 524320 | tf_op jit(solution)/shard_map/ppermute | solution.py:116
  116.8 11.2 %collective-permute-done.28 = bf16[512,512]{1,0:T(8,128)(2,1)S(1)} collective-permute-done((bf16[512,512]{1,0:T(8,128)(2,1)}, bf16[512,512]{1,0:T(8,128)(2,1)S(1)}, u32[]{:S(2)}, u32[]{:S(2)}) %collective-permute-start.28) | collective-permute-done | bytes 524320 | tf_op jit(solution)/shard_map/ppermute | solution.py:116
  138.2 4.4 collective-permute-start.12
  145.1 10.7 %collective-permute-done.10 = bf16[2,64,2048]{2,1,0:T(8,128)(2,1)S(1)} collective-permute-done((bf16[2,64,2048]{2,1,0:T(8,128)(2,1)S(1)}, bf16[2,64,2048]{2,1,0:T(8,128)(2,1)S(1)}, u32[]{:S(2)}, u32[]{:S(2)}) %collective-permute-start.10) | collective-permute-done | bytes 524320 | tf_op jit(solution)/shard_map/ppermute | solution.py:119
  158.4 7.7 collective-permute-done.12
  167.7 19.5 %collective-permute-done.13 = bf16[2,64,2048]{2,1,0:T(8,128)(2,1)S(1)} collective-permute-done((bf16[2,64,2048]{2,1,0:T(8,128)(2,1)S(1)}, bf16[2,64,2048]{2,1,0:T(8,128)(2,1)S(1)}, u32[]{:S(2)}, u32[]{:S(2)}) %collective-permute-start.13) | collective-permute-done | bytes 524320 | tf_op jit(solution)/shard_map/ppermute | solution.py:119
  192.6 11.2 %collective-permute-done.5 = bf16[4,64,2048]{2,1,0:T(8,128)(2,1)S(1)} collective-permute-done((bf16[4,64,2048]{2,1,0:T(8,128)(2,1)S(1)}, bf16[4,64,2048]{2,1,0:T(8,128)(2,1)S(1)}, u32[]{:S(2)}, u32[]{:S(2)}) %collective-permute-start.5) | collective-permute-done | bytes 1048608 | tf_op jit(solution)/shard_map/ppermute | solution.py:116
  215.3 10.6 %fusion.163 = (f32[4,1024]{1,0:T(4,128)S(1)}, f32[4,1024,1024]{1,2,0:T(8,128)}) fusion(pred[1024,1024]{0,1:T(8,128)(4,1)} %compare_and_fusion, bf16[1024,4,32]{0,2,1:T(8,128)(2,1)} %get-tuple-element.57, bf16[1024,4,32]{0,2,1:T(8,128)(2,1)} %get-tuple-element.56, bf16[1024,32]{0,1:T(8,128)(2,1)S(1)} %get-tuple-element.86, ...), kind=kOutput, calls=%fused_computation.382 | convolution fusion | flops 554959872 | bytes 18497536 | tf_op jit(solution)/shard_map/sub | solution.py:343
  225.9 8.2 fusion.37
  243.6 7.9 all-to-all-start
  258.5 5.2 all-to-all-done
  295.2 4.1 collective-permute-done.20
  303.6 4.4 collective-permute-done.38
  309.4 3.9 collective-permute-start.41
  326.7 11.9 %collective-permute-done.24 = bf16[4,64,2048]{2,1,0:T(8,128)(2,1)} collective-permute-done((bf16[4,64,2048]{2,1,0:T(8,128)(2,1)}, bf16[4,64,2048]{2,1,0:T(8,128)(2,1)}, u32[]{:S(2)}, u32[]{:S(2)}) %collective-permute-start.24) | collective-permute-done | bytes 1048608 | tf_op jit(solution)/shard_map/ppermute | solution.py:116
  341.5 5.8 collective-permute-done.42
  351.4 8.3 reverse_select_fusion.3
  369.1 20.1 %collective-permute-done.25 = bf16[2,4,64,2048]{3,2,1,0:T(8,128)(2,1)} collective-permute-done((bf16[2,4,64,2048]{3,2,1,0:T(8,128)(2,1)}, bf16[2,4,64,2048]{3,2,1,0:T(8,128)(2,1)}, u32[]{:S(2)}, u32[]{:S(2)}) %collective-permute-start.25) | collective-permute-done | bytes 2097184 | tf_op jit(solution)/shard_map/ppermute | solution.py:116
  400.4 4.1 fusion.166
  404.5 4.3 multiply_convert_fusion.2
  408.7 4.4 fusion.179
  418.9 4.7 fusion.178
  426.0 5.8 fusion.168
  444.9 7.5 add_convert_fusion.1
  456.1 5.8 fusion.169
  461.9 6.1 add_convert_fusion
  471.8 13.3 %collective-permute-done.32 = bf16[2,4,64,2048]{3,2,1,0:T(8,128)(2,1)S(1)} collective-permute-done((bf16[2,4,64,2048]{3,2,1,0:T(8,128)(2,1)}, bf16[2,4,64,2048]{3,2,1,0:T(8,128)(2,1)S(1)}, u32[]{:S(2)}, u32[]{:S(2)}) %collective-permute-start.32) | collective-permute-done | bytes 2097184 | tf_op jit(solution)/shard_map/ppermute | solution.py:116
  492.4 37.8 %collective-permute-done.49 = bf16[2,4,64,2048]{3,2,1,0:T(8,128)(2,1)} collective-permute-done((bf16[2,4,64,2048]{3,2,1,0:T(8,128)(2,1)}, bf16[2,4,64,2048]{3,2,1,0:T(8,128)(2,1)}, u32[]{:S(2)}, u32[]{:S(2)}) %collective-permute-start.49) | collective-permute-done | bytes 2097184 | tf_op jit(solution)/shard_map/ppermute | solution.py:116
  537.5 16.9 %collective-permute-done.33 = bf16[4,64,2048]{2,1,0:T(8,128)(2,1)S(1)} collective-permute-done((bf16[4,64,2048]{2,1,0:T(8,128)(2,1)S(1)}, bf16[4,64,2048]{2,1,0:T(8,128)(2,1)S(1)}, u32[]{:S(2)}, u32[]{:S(2)}) %collective-permute-start.33) | collective-permute-done | bytes 1048608 | tf_op jit(solution)/shard_map/ppermute | solution.py:116
  555.3 5.8 collective-permute-done.45
  561.7 14.0 %collective-permute-done.50 = bf16[4,64,2048]{2,1,0:T(8,128)(2,1)S(1)} collective-permute-done((bf16[4,64,2048]{2,1,0:T(8,128)(2,1)S(1)}, bf16[4,64,2048]{2,1,0:T(8,128)(2,1)S(1)}, u32[]{:S(2)}, u32[]{:S(2)}) %collective-permute-start.50) | collective-permute-done | bytes 1048608 | tf_op jit(solution)/shard_map/ppermute | solution.py:116
  577.3 5.0 collective-permute-done.55
  584.1 7.3 collective-permute-done.34
  593.0 9.7 %collective-permute-done.46 = bf16[2,64,2048]{2,1,0:T(8,128)(2,1)S(1)} collective-permute-done((bf16[2,64,2048]{2,1,0:T(8,128)(2,1)S(1)}, bf16[2,64,2048]{2,1,0:T(8,128)(2,1)S(1)}, u32[]{:S(2)}, u32[]{:S(2)}) %collective-permute-start.46) | collective-permute-done | bytes 524320 | tf_op jit(solution)/shard_map/ppermute | solution.py:119
  604.7 9.2 collective-permute-done.51
  616.3 4.3 collective-permute-done.56
  622.8 6.5 collective-permute-done.35
  631.6 9.0 collective-permute-done.47
  642.8 9.0 collective-permute-done.52
  652.0 6.7 collective-permute-done.57
  658.8 9.0 collective-permute-done.36
  668.0 8.2 collective-permute-done.53
  676.5 7.1 collective-permute-done.58
  685.2 4.8 collective-permute-done.48
  701.5 4.2 all-to-all-start.1
  705.7 6.1 convolution_add_fusion
  722.4 7.2 all-to-all-start.6
  731.3 7.6 fusion.1
  738.9 7.9 fusion.3
  753.1 6.1 fusion.44
  760.1 11.5 %all-to-all-done.6 = bf16[16,64,512]{2,1,0:T(8,128)(2,1)S(1)} async-done(((bf16[16,64,512]{2,1,0:T(8,128)(2,1)}), bf16[16,64,512]{2,1,0:T(8,128)(2,1)S(1)}, u32[]{:S(2)}, u32[]{:S(2)}) %all-to-all-start.6) | async-done | bytes 1048608 | tf_op jit(solution)/shard_map/all_to_all | solution.py:428
  771.7 5.6 all-to-all-start.5
  777.2 9.2 fusion.48
  789.9 39.1 %all-to-all-done.5 = bf16[16,64,512]{2,1,0:T(8,128)(2,1)S(1)} async-done(((bf16[16,64,512]{2,1,0:T(8,128)(2,1)}), bf16[16,64,512]{2,1,0:T(8,128)(2,1)S(1)}, u32[]{:S(2)}, u32[]{:S(2)}) %all-to-all-start.5) | async-done | bytes 1048608 | tf_op jit(solution)/shard_map/all_to_all | solution.py:428
  829.0 5.4 all-to-all-start.2
  834.3 3.9 bitcast_add_fusion.2
  842.8 4.0 fusion.20
  875.9 3.6 fusion.10
  881.5 6.4 all-to-all-start.3
  890.4 4.2 collective-permute-done.69
  896.7 6.7 all-to-all-start.4
  911.8 8.4 all-to-all-done.4
  (544 shorter events, 310.7 us)
Async XLA Ops:
  7.2 344.2 %all-gather.7.cloned.1.call-start = ((), (), s32[]{:S(2)}) async-start(), calls=%async_computation.8 | async-start | bytes 4456448 | tf_op jit(solution)/shard_map/all_gather | solution.py:217
  9.2 342.2 %all-gather.5.cloned.1.call-start = ((), (), s32[]{:S(2)}) async-start(), calls=%async_computation.7 | async-start | bytes 4456448 | tf_op jit(solution)/shard_map/all_gather | solution.py:217
  11.2 27.3 %collective-permute-start = (bf16[64,2048]{1,0:T(8,128)(2,1)}, bf16[64,2048]{1,0:T(8,128)(2,1)}, u32[]{:S(2)}, u32[]{:S(2)}) collective-permute-start(bf16[64,2048]{1,0:T(8,128)(2,1)} %get-tuple-element.78), channel_id=1, source_target_pairs={{0,8},{1,9},{2,10},{3,11},{4,12},{5,13},{6,14},{7,15},{8,0},{9,1},... | collective-permute-start | bytes 786440 | tf_op jit(solution)/shard_map/ppermute | solution.py:116
  11.7 27.4 %collective-permute-start.2 = (bf16[64,2048]{1,0:T(8,128)(2,1)}, bf16[64,2048]{1,0:T(8,128)(2,1)}, u32[]{:S(2)}, u32[]{:S(2)}) collective-permute-start(bf16[64,2048]{1,0:T(8,128)(2,1)} %get-tuple-element.78), channel_id=1, source_target_pairs={{8,16},{9,17},{10,18},{11,19},{12,20},{13,21},{14,22},{15,23},{16,... | collective-permute-start | bytes 786440 | tf_op jit(solution)/shard_map/ppermute | solution.py:119
  16.3 19.6 %collective-permute-start.8 = (bf16[64,2048]{1,0:T(8,128)(2,1)}, bf16[64,2048]{1,0:T(8,128)(2,1)}, u32[]{:S(2)}, u32[]{:S(2)}) collective-permute-start(bf16[64,2048]{1,0:T(8,128)(2,1)} %get-tuple-element.79), channel_id=1, source_target_pairs={{0,4},{1,5},{2,6},{3,7},{4,0},{5,1},{6,2},{7,3},{8,12},{9,13},{10,... | collective-permute-start | bytes 786440 | tf_op jit(solution)/shard_map/ppermute | solution.py:116
  16.9 14.6 %collective-permute-start.6 = (bf16[512,2]{0,1:T(2,128)(2,1)S(1)}, bf16[512,2]{0,1:T(2,128)(2,1)S(1)}, u32[]{:S(2)}, u32[]{:S(2)}) collective-permute-start(bf16[512,2]{0,1:T(2,128)(2,1)S(1)} %pad_maximum_fusion.35), channel_id=1, source_target_pairs={{0,2},{1,3},{2,0},{3,1},{4,6},{5,7},{6,4},{7,5},{8,10},{9,11},{10,... | collective-permute-start | bytes 6152 | tf_op jit(solution)/shard_map/ppermute | solution.py:116
  21.4 19.6 %collective-permute-start.14 = (bf16[512,384]{1,0:T(8,128)(2,1)}, bf16[512,384]{1,0:T(8,128)(2,1)}, u32[]{:S(2)}, u32[]{:S(2)}) collective-permute-start(bf16[512,384]{1,0:T(8,128)(2,1)} %pad_maximum_fusion.26), channel_id=1, source_target_pairs={{0,2},{1,3},{2,0},{3,1},{4,6},{5,7},{6,4},{7,5},{8,10},{9,11},{10,... | collective-permute-start | bytes 1179656 | tf_op jit(solution)/shard_map/ppermute | solution.py:116
  34.7 217.5 %collective-permute-start.17 = (bf16[512,2048]{1,0:T(8,128)(2,1)S(1)}, bf16[512,2048]{1,0:T(8,128)(2,1)}, u32[]{:S(2)}, u32[]{:S(2)}) collective-permute-start(bf16[512,2048]{1,0:T(8,128)(2,1)S(1)} %copy-done.11), channel_id=1, source_target_pairs={{0,2},{1,3},{2,0},{3,1},{4,6},{5,7},{6,4},{7,5},{8,10},{9,11},{10,... | collective-permute-start | bytes 6291464 | tf_op jit(solution)/shard_map/ppermute | solution.py:116
  35.9 80.9 %collective-permute-start.26 = (bf16[512,512]{1,0:T(8,128)(2,1)}, bf16[512,512]{1,0:T(8,128)(2,1)S(1)}, u32[]{:S(2)}, u32[]{:S(2)}) collective-permute-start(bf16[512,512]{1,0:T(8,128)(2,1)} %constant_dynamic-slice_fusion.2), channel_id=1, source_target_pairs={{0,2},{1,3},{2,0},{3,1},{4,6},{5,7},{6,4},{7,5},{8,10},{9,11},{10,... | collective-permute-start | bytes 1572872 | tf_op jit(solution)/shard_map/ppermute | solution.py:116
  38.5 89.5 %collective-permute-start.28 = (bf16[512,512]{1,0:T(8,128)(2,1)}, bf16[512,512]{1,0:T(8,128)(2,1)S(1)}, u32[]{:S(2)}, u32[]{:S(2)}) collective-permute-start(bf16[512,512]{1,0:T(8,128)(2,1)} %constant_dynamic-slice_fusion.1), channel_id=1, source_target_pairs={{0,2},{1,3},{2,0},{3,1},{4,6},{5,7},{6,4},{7,5},{8,10},{9,11},{10,... | collective-permute-start | bytes 1572872 | tf_op jit(solution)/shard_map/ppermute | solution.py:116
  39.1 14.9 %collective-permute-start.1 = (bf16[64,2048]{1,0:T(8,128)(2,1)}, bf16[64,2048]{1,0:T(8,128)(2,1)S(1)}, u32[]{:S(2)}, u32[]{:S(2)}) collective-permute-start(bf16[64,2048]{1,0:T(8,128)(2,1)} %collective-permute-done), channel_id=1, source_target_pairs={{8,16},{9,17},{10,18},{11,19},{12,20},{13,21},{14,22},{15,23},{16,... | collective-permute-start | bytes 786440 | tf_op jit(solution)/shard_map/ppermute | solution.py:119
  54.0 78.8 %collective-permute-start.9 = (bf16[2,64,2048]{2,1,0:T(8,128)(2,1)S(1)}, bf16[2,64,2048]{2,1,0:T(8,128)(2,1)S(1)}, u32[]{:S(2)}, u32[]{:S(2)}) collective-permute-start(bf16[2,64,2048]{2,1,0:T(8,128)(2,1)S(1)} %get-tuple-element.82), channel_id=1, source_target_pairs={{0,8},{1,9},{2,10},{3,11},{4,12},{5,13},{6,14},{7,15},{8,0},{9,1},... | collective-permute-start | bytes 1572872 | tf_op jit(solution)/shard_map/ppermute | solution.py:116
  54.0 78.8 %collective-permute-start.11 = (bf16[2,64,2048]{2,1,0:T(8,128)(2,1)S(1)}, bf16[2,64,2048]{2,1,0:T(8,128)(2,1)S(1)}, u32[]{:S(2)}, u32[]{:S(2)}) collective-permute-start(bf16[2,64,2048]{2,1,0:T(8,128)(2,1)S(1)} %get-tuple-element.82), channel_id=1, source_target_pairs={{8,16},{9,17},{10,18},{11,19},{12,20},{13,21},{14,22},{15,23},{16,... | collective-permute-start | bytes 1572872 | tf_op jit(solution)/shard_map/ppermute | solution.py:119
  116.8 28.0 %collective-permute-start.15 = (bf16[2,512,384]{2,1,0:T(8,128)(2,1)S(1)}, bf16[2,512,384]{2,1,0:T(8,128)(2,1)S(1)}, u32[]{:S(2)}, u32[]{:S(2)}) collective-permute-start(bf16[2,512,384]{2,1,0:T(8,128)(2,1)S(1)} %pad_maximum_fusion.17), channel_id=1, source_target_pairs={{0,1},{1,0},{2,3},{3,2},{4,5},{5,4},{6,7},{7,6},{8,9},{9,8},{10,11... | collective-permute-start | bytes 2359304 | tf_op jit(solution)/shard_map/ppermute | solution.py:116
  132.8 136.9 %collective-permute-start.16 = (bf16[512,2048]{1,0:T(8,128)(2,1)S(1)}, bf16[512,2048]{1,0:T(8,128)(2,1)}, u32[]{:S(2)}, u32[]{:S(2)}) collective-permute-start(bf16[512,2048]{1,0:T(8,128)(2,1)S(1)} %copy-done.11), channel_id=1, source_target_pairs={{0,1},{1,0},{2,3},{3,2},{4,5},{5,4},{6,7},{7,6},{8,9},{9,8},{10,11... | collective-permute-start | bytes 6291464 | tf_op jit(solution)/shard_map/ppermute | solution.py:116
  132.8 22.9 %collective-permute-start.10 = (bf16[2,64,2048]{2,1,0:T(8,128)(2,1)S(1)}, bf16[2,64,2048]{2,1,0:T(8,128)(2,1)S(1)}, u32[]{:S(2)}, u32[]{:S(2)}) collective-permute-start(bf16[2,64,2048]{2,1,0:T(8,128)(2,1)S(1)} %collective-permute-done.9), channel_id=1, source_target_pairs={{8,16},{9,17},{10,18},{11,19},{12,20},{13,21},{14,22},{15,23},{16,... | collective-permute-start | bytes 1572872 | tf_op jit(solution)/shard_map/ppermute | solution.py:119
  138.2 27.9 %collective-permute-start.12 = (bf16[2,64,2048]{2,1,0:T(8,128)(2,1)S(1)}, bf16[2,64,2048]{2,1,0:T(8,128)(2,1)S(1)}, u32[]{:S(2)}, u32[]{:S(2)}) collective-permute-start(bf16[2,64,2048]{2,1,0:T(8,128)(2,1)S(1)} %collective-permute-done.11), channel_id=1, source_target_pairs={{8,0},{9,1},{10,2},{11,3},{12,4},{13,5},{14,6},{15,7},{16,24},{17,... | collective-permute-start | bytes 1572872 | tf_op jit(solution)/shard_map/ppermute | solution.py:119
  144.8 707.3 %collective-permute-start.60 = (bf16[512,512]{1,0:T(8,128)(2,1)}, bf16[512,512]{1,0:T(8,128)(2,1)}, u32[]{:S(2)}, u32[]{:S(2)}) collective-permute-start(bf16[512,512]{1,0:T(8,128)(2,1)} %param.19), channel_id=1, source_target_pairs={{0,1},{1,0},{2,3},{3,2},{4,5},{5,4},{6,7},{7,6},{8,9},{9,8},{10,11... | collective-permute-start | bytes 1572872 | tf_op jit(solution)/shard_map/ppermute | solution.py:116
  155.7 31.4 %collective-permute-start.13 = (bf16[2,64,2048]{2,1,0:T(8,128)(2,1)S(1)}, bf16[2,64,2048]{2,1,0:T(8,128)(2,1)S(1)}, u32[]{:S(2)}, u32[]{:S(2)}) collective-permute-start(bf16[2,64,2048]{2,1,0:T(8,128)(2,1)S(1)} %collective-permute-done.10), channel_id=1, source_target_pairs={{8,0},{9,1},{10,2},{11,3},{12,4},{13,5},{14,6},{15,7},{16,24},{17,... | collective-permute-start | bytes 1572872 | tf_op jit(solution)/shard_map/ppermute | solution.py:119
  166.1 37.7 %collective-permute-start.5 = (bf16[4,64,2048]{2,1,0:T(8,128)(2,1)S(1)}, bf16[4,64,2048]{2,1,0:T(8,128)(2,1)S(1)}, u32[]{:S(2)}, u32[]{:S(2)}) collective-permute-start(bf16[4,64,2048]{2,1,0:T(8,128)(2,1)S(1)} %get-tuple-element.64), channel_id=1, source_target_pairs={{0,4},{1,5},{2,6},{3,7},{4,0},{5,1},{6,2},{7,3},{8,12},{9,13},{10,... | collective-permute-start | bytes 3145736 | tf_op jit(solution)/shard_map/ppermute | solution.py:116
  187.2 95.4 %collective-permute-start.30 = (bf16[512,2048]{1,0:T(8,128)(2,1)}, bf16[512,2048]{1,0:T(8,128)(2,1)}, u32[]{:S(2)}, u32[]{:S(2)}) collective-permute-start(bf16[512,2048]{1,0:T(8,128)(2,1)} %constant_dynamic-slice_fusion), channel_id=1, source_target_pairs={{0,2},{4,6},{9,11},{13,15},{18,16},{22,20},{27,25},{31,29}} | collective-permute-start | bytes 6291464 | tf_op jit(solution)/shard_map/ppermute | solution.py:119
  203.8 51.4 %collective-permute-start.29 = (bf16[2,512,512]{2,1,0:T(8,128)(2,1)}, bf16[2,512,512]{2,1,0:T(8,128)(2,1)}, u32[]{:S(2)}, u32[]{:S(2)}) collective-permute-start(bf16[2,512,512]{2,1,0:T(8,128)(2,1)} %pad_maximum_fusion.13), channel_id=1, source_target_pairs={{0,1},{1,0},{2,3},{3,2},{4,5},{5,4},{6,7},{7,6},{8,9},{9,8},{10,11... | collective-permute-start | bytes 3145736 | tf_op jit(solution)/shard_map/ppermute | solution.py:116
  243.6 20.2 %all-to-all-start = ((bf16[8,128,256]{2,1,0:T(8,128)(2,1)}), bf16[8,128,256]{2,1,0:T(8,128)(2,1)}, u32[]{:S(2)}, u32[]{:S(2)}) async-start(bf16[8,128,256]{2,1,0:T(8,128)(2,1)} %bitcast.478), calls=%async_computation | async-start | bytes 1048576 | tf_op jit(solution)/shard_map/all_to_all | solution.py:353
  252.2 19.7 %collective-permute-start.18 = (bf16[512,2048]{1,0:T(8,128)(2,1)}, bf16[512,2048]{1,0:T(8,128)(2,1)}, u32[]{:S(2)}, u32[]{:S(2)}) collective-permute-start(bf16[512,2048]{1,0:T(8,128)(2,1)} %collective-permute-done.17), channel_id=1, source_target_pairs={{0,1},{1,0},{2,3},{3,2},{4,5},{5,4},{6,7},{7,6},{8,9},{9,8},{10,11... | collective-permute-start | bytes 6291464 | tf_op jit(solution)/shard_map/ppermute | solution.py:116
  255.2 25.9 %collective-permute-start.27 = (bf16[2,512,512]{2,1,0:T(8,128)(2,1)}, bf16[2,512,512]{2,1,0:T(8,128)(2,1)}, u32[]{:S(2)}, u32[]{:S(2)}) collective-permute-start(bf16[2,512,512]{2,1,0:T(8,128)(2,1)} %pad_maximum_fusion.12), channel_id=1, source_target_pairs={{0,1},{1,0},{2,3},{3,2},{4,5},{5,4},{6,7},{7,6},{8,9},{9,8},{10,11... | collective-permute-start | bytes 3145736 | tf_op jit(solution)/shard_map/ppermute | solution.py:116
  293.9 564.4 %collective-permute-start.61 = (bf16[512,512]{1,0:T(8,128)(2,1)}, bf16[512,512]{1,0:T(8,128)(2,1)}, u32[]{:S(2)}, u32[]{:S(2)}) collective-permute-start(bf16[512,512]{1,0:T(8,128)(2,1)} %param.20), channel_id=1, source_target_pairs={{0,1},{1,0},{2,3},{3,2},{4,5},{5,4},{6,7},{7,6},{8,9},{9,8},{10,11... | collective-permute-start | bytes 1572872 | tf_op jit(solution)/shard_map/ppermute | solution.py:116
  295.2 28.3 %collective-permute-start.31 = (bf16[512,2048]{1,0:T(8,128)(2,1)S(1)}, bf16[512,2048]{1,0:T(8,128)(2,1)}, u32[]{:S(2)}, u32[]{:S(2)}) collective-permute-start(bf16[512,2048]{1,0:T(8,128)(2,1)S(1)} %dynamic-slice_select_fusion), channel_id=1, source_target_pairs={{0,1},{1,0},{2,3},{3,2},{4,5},{5,4},{6,7},{7,6},{8,9},{9,8},{10,11... | collective-permute-start | bytes 6291464 | tf_op jit(solution)/shard_map/ppermute | solution.py:116
  317.5 21.1 %collective-permute-start.24 = (bf16[4,64,2048]{2,1,0:T(8,128)(2,1)}, bf16[4,64,2048]{2,1,0:T(8,128)(2,1)}, u32[]{:S(2)}, u32[]{:S(2)}) collective-permute-start(bf16[4,64,2048]{2,1,0:T(8,128)(2,1)} %get-tuple-element.60), channel_id=1, source_target_pairs={{0,4},{1,5},{2,6},{3,7},{4,0},{5,1},{6,2},{7,3},{8,12},{9,13},{10,... | collective-permute-start | bytes 3145736 | tf_op jit(solution)/shard_map/ppermute | solution.py:116
  320.9 26.3 %collective-permute-start.42 = (bf16[4,64,2048]{2,1,0:T(8,128)(2,1)}, bf16[4,64,2048]{2,1,0:T(8,128)(2,1)}, u32[]{:S(2)}, u32[]{:S(2)}) collective-permute-start(bf16[4,64,2048]{2,1,0:T(8,128)(2,1)} %get-tuple-element.62), channel_id=1, source_target_pairs={{0,2},{1,3},{2,0},{3,1},{4,6},{5,7},{6,4},{7,5},{8,10},{9,11},{10,... | collective-permute-start | bytes 3145736 | tf_op jit(solution)/shard_map/ppermute | solution.py:116
  341.5 47.6 %collective-permute-start.25 = (bf16[2,4,64,2048]{3,2,1,0:T(8,128)(2,1)}, bf16[2,4,64,2048]{3,2,1,0:T(8,128)(2,1)}, u32[]{:S(2)}, u32[]{:S(2)}) collective-permute-start(bf16[2,4,64,2048]{3,2,1,0:T(8,128)(2,1)} %get-tuple-element.45), channel_id=1, source_target_pairs={{0,2},{1,3},{2,0},{3,1},{4,6},{5,7},{6,4},{7,5},{8,10},{9,11},{10,... | collective-permute-start | bytes 6291464 | tf_op jit(solution)/shard_map/ppermute | solution.py:116
  350.8 45.3 %collective-permute-start.43 = (bf16[2,4,64,2048]{3,2,1,0:T(8,128)(2,1)}, bf16[2,4,64,2048]{3,2,1,0:T(8,128)(2,1)}, u32[]{:S(2)}, u32[]{:S(2)}) collective-permute-start(bf16[2,4,64,2048]{3,2,1,0:T(8,128)(2,1)} %get-tuple-element.51), channel_id=1, source_target_pairs={{0,4},{1,5},{2,6},{3,7},{4,0},{5,1},{6,2},{7,3},{8,12},{9,13},{10,... | collective-permute-start | bytes 6291464 | tf_op jit(solution)/shard_map/ppermute | solution.py:116
  436.4 48.7 %collective-permute-start.32 = (bf16[2,4,64,2048]{3,2,1,0:T(8,128)(2,1)}, bf16[2,4,64,2048]{3,2,1,0:T(8,128)(2,1)S(1)}, u32[]{:S(2)}, u32[]{:S(2)}) collective-permute-start(bf16[2,4,64,2048]{3,2,1,0:T(8,128)(2,1)} %bitcast.70), channel_id=1, source_target_pairs={{0,2},{1,3},{2,0},{3,1},{4,6},{5,7},{6,4},{7,5},{8,10},{9,11},{10,... | collective-permute-start | bytes 6291464 | tf_op jit(solution)/shard_map/ppermute | solution.py:116
  441.0 48.7 %collective-permute-start.44 = (bf16[2,4,64,2048]{3,2,1,0:T(8,128)(2,1)}, bf16[2,4,64,2048]{3,2,1,0:T(8,128)(2,1)S(1)}, u32[]{:S(2)}, u32[]{:S(2)}) collective-permute-start(bf16[2,4,64,2048]{3,2,1,0:T(8,128)(2,1)} %bitcast.85), channel_id=1, source_target_pairs={{0,4},{1,5},{2,6},{3,7},{4,0},{5,1},{6,2},{7,3},{8,12},{9,13},{10,... | collective-permute-start | bytes 6291464 | tf_op jit(solution)/shard_map/ppermute | solution.py:116
  454.3 75.9 %collective-permute-start.49 = (bf16[2,4,64,2048]{3,2,1,0:T(8,128)(2,1)}, bf16[2,4,64,2048]{3,2,1,0:T(8,128)(2,1)}, u32[]{:S(2)}, u32[]{:S(2)}) collective-permute-start(bf16[2,4,64,2048]{3,2,1,0:T(8,128)(2,1)} %bitcast.96), channel_id=1, source_target_pairs={{0,2},{1,3},{2,0},{3,1},{4,6},{5,7},{6,4},{7,5},{8,10},{9,11},{10,... | collective-permute-start | bytes 6291464 | tf_op jit(solution)/shard_map/ppermute | solution.py:116
  485.1 49.5 %collective-permute-start.54 = (bf16[2,4,64,2048]{3,2,1,0:T(8,128)(2,1)S(1)}, bf16[2,4,64,2048]{3,2,1,0:T(8,128)(2,1)S(1)}, u32[]{:S(2)}, u32[]{:S(2)}) collective-permute-start(bf16[2,4,64,2048]{3,2,1,0:T(8,128)(2,1)S(1)} %bitcast.534), channel_id=1, source_target_pairs={{0,4},{1,5},{2,6},{3,7},{4,0},{5,1},{6,2},{7,3},{8,12},{9,13},{10,... | collective-permute-start | bytes 6291464 | tf_op jit(solution)/shard_map/ppermute | solution.py:116
  489.7 361.0 %collective-permute-start.63 = (bf16[512,512]{1,0:T(8,128)(2,1)}, bf16[512,512]{1,0:T(8,128)(2,1)}, u32[]{:S(2)}, u32[]{:S(2)}) collective-permute-start(bf16[512,512]{1,0:T(8,128)(2,1)} %param.19), channel_id=1, source_target_pairs={{0,2},{1,3},{2,0},{3,1},{4,6},{5,7},{6,4},{7,5},{8,10},{9,11},{10,... | collective-permute-start | bytes 1572872 | tf_op jit(solution)/shard_map/ppermute | solution.py:116
  530.2 24.2 %collective-permute-start.33 = (bf16[4,64,2048]{2,1,0:T(8,128)(2,1)S(1)}, bf16[4,64,2048]{2,1,0:T(8,128)(2,1)S(1)}, u32[]{:S(2)}, u32[]{:S(2)}) collective-permute-start(bf16[4,64,2048]{2,1,0:T(8,128)(2,1)S(1)} %fusion.51), channel_id=1, source_target_pairs={{0,4},{1,5},{2,6},{3,7},{4,0},{5,1},{6,2},{7,3},{8,12},{9,13},{10,... | collective-permute-start | bytes 3145736 | tf_op jit(solution)/shard_map/ppermute | solution.py:116
  534.7 26.4 %collective-permute-start.45 = (bf16[4,64,2048]{2,1,0:T(8,128)(2,1)S(1)}, bf16[4,64,2048]{2,1,0:T(8,128)(2,1)S(1)}, u32[]{:S(2)}, u32[]{:S(2)}) collective-permute-start(bf16[4,64,2048]{2,1,0:T(8,128)(2,1)S(1)} %fusion.52), channel_id=1, source_target_pairs={{0,2},{1,3},{2,0},{3,1},{4,6},{5,7},{6,4},{7,5},{8,10},{9,11},{10,... | collective-permute-start | bytes 3145736 | tf_op jit(solution)/shard_map/ppermute | solution.py:116
  554.4 21.3 %collective-permute-start.50 = (bf16[4,64,2048]{2,1,0:T(8,128)(2,1)S(1)}, bf16[4,64,2048]{2,1,0:T(8,128)(2,1)S(1)}, u32[]{:S(2)}, u32[]{:S(2)}) collective-permute-start(bf16[4,64,2048]{2,1,0:T(8,128)(2,1)S(1)} %fusion.53), channel_id=1, source_target_pairs={{0,4},{1,5},{2,6},{3,7},{4,0},{5,1},{6,2},{7,3},{8,12},{9,13},{10,... | collective-permute-start | bytes 3145736 | tf_op jit(solution)/shard_map/ppermute | solution.py:116
  561.1 21.2 %collective-permute-start.55 = (bf16[4,64,2048]{2,1,0:T(8,128)(2,1)S(1)}, bf16[4,64,2048]{2,1,0:T(8,128)(2,1)S(1)}, u32[]{:S(2)}, u32[]{:S(2)}) collective-permute-start(bf16[4,64,2048]{2,1,0:T(8,128)(2,1)S(1)} %fusion.54), channel_id=1, source_target_pairs={{0,2},{1,3},{2,0},{3,1},{4,6},{5,7},{6,4},{7,5},{8,10},{9,11},{10,... | collective-permute-start | bytes 3145736 | tf_op jit(solution)/shard_map/ppermute | solution.py:116
  575.7 15.7 %collective-permute-start.34 = (bf16[2,64,2048]{2,1,0:T(8,128)(2,1)S(1)}, bf16[2,64,2048]{2,1,0:T(8,128)(2,1)S(1)}, u32[]{:S(2)}, u32[]{:S(2)}) collective-permute-start(bf16[2,64,2048]{2,1,0:T(8,128)(2,1)S(1)} %stack.321), channel_id=1, source_target_pairs={{0,8},{1,9},{2,10},{3,11},{4,12},{5,13},{6,14},{7,15},{24,16},{25,... | collective-permute-start | bytes 1572872 | tf_op jit(solution)/shard_map/ppermute | solution.py:119
  582.3 20.3 %collective-permute-start.46 = (bf16[2,64,2048]{2,1,0:T(8,128)(2,1)S(1)}, bf16[2,64,2048]{2,1,0:T(8,128)(2,1)S(1)}, u32[]{:S(2)}, u32[]{:S(2)}) collective-permute-start(bf16[2,64,2048]{2,1,0:T(8,128)(2,1)S(1)} %stack.320), channel_id=1, source_target_pairs={{0,8},{1,9},{2,10},{3,11},{4,12},{5,13},{6,14},{7,15},{24,16},{25,... | collective-permute-start | bytes 1572872 | tf_op jit(solution)/shard_map/ppermute | solution.py:119
  591.4 22.5 %collective-permute-start.51 = (bf16[2,64,2048]{2,1,0:T(8,128)(2,1)S(1)}, bf16[2,64,2048]{2,1,0:T(8,128)(2,1)S(1)}, u32[]{:S(2)}, u32[]{:S(2)}) collective-permute-start(bf16[2,64,2048]{2,1,0:T(8,128)(2,1)S(1)} %stack.319), channel_id=1, source_target_pairs={{0,8},{1,9},{2,10},{3,11},{4,12},{5,13},{6,14},{7,15},{24,16},{25,... | collective-permute-start | bytes 1572872 | tf_op jit(solution)/shard_map/ppermute | solution.py:119
  602.7 17.9 %collective-permute-start.56 = (bf16[2,64,2048]{2,1,0:T(8,128)(2,1)S(1)}, bf16[2,64,2048]{2,1,0:T(8,128)(2,1)S(1)}, u32[]{:S(2)}, u32[]{:S(2)}) collective-permute-start(bf16[2,64,2048]{2,1,0:T(8,128)(2,1)S(1)} %stack.318), channel_id=1, source_target_pairs={{0,8},{1,9},{2,10},{3,11},{4,12},{5,13},{6,14},{7,15},{24,16},{25,... | collective-permute-start | bytes 1572872 | tf_op jit(solution)/shard_map/ppermute | solution.py:119
  613.9 15.4 %collective-permute-start.35 = (bf16[2,64,2048]{2,1,0:T(8,128)(2,1)S(1)}, bf16[2,64,2048]{2,1,0:T(8,128)(2,1)S(1)}, u32[]{:S(2)}, u32[]{:S(2)}) collective-permute-start(bf16[2,64,2048]{2,1,0:T(8,128)(2,1)S(1)} %pad_maximum_fusion.21), channel_id=1, source_target_pairs={{8,16},{9,17},{10,18},{11,19},{12,20},{13,21},{14,22},{15,23},{16,... | collective-permute-start | bytes 1572872 | tf_op jit(solution)/shard_map/ppermute | solution.py:119
  620.6 20.0 %collective-permute-start.47 = (bf16[2,64,2048]{2,1,0:T(8,128)(2,1)S(1)}, bf16[2,64,2048]{2,1,0:T(8,128)(2,1)S(1)}, u32[]{:S(2)}, u32[]{:S(2)}) collective-permute-start(bf16[2,64,2048]{2,1,0:T(8,128)(2,1)S(1)} %pad_maximum_fusion.22), channel_id=1, source_target_pairs={{8,16},{9,17},{10,18},{11,19},{12,20},{13,21},{14,22},{15,23},{16,... | collective-permute-start | bytes 1572872 | tf_op jit(solution)/shard_map/ppermute | solution.py:119
  629.3 22.5 %collective-permute-start.52 = (bf16[2,64,2048]{2,1,0:T(8,128)(2,1)S(1)}, bf16[2,64,2048]{2,1,0:T(8,128)(2,1)S(1)}, u32[]{:S(2)}, u32[]{:S(2)}) collective-permute-start(bf16[2,64,2048]{2,1,0:T(8,128)(2,1)S(1)} %pad_maximum_fusion.23), channel_id=1, source_target_pairs={{8,16},{9,17},{10,18},{11,19},{12,20},{13,21},{14,22},{15,23},{16,... | collective-permute-start | bytes 1572872 | tf_op jit(solution)/shard_map/ppermute | solution.py:119
  640.5 18.1 %collective-permute-start.57 = (bf16[2,64,2048]{2,1,0:T(8,128)(2,1)S(1)}, bf16[2,64,2048]{2,1,0:T(8,128)(2,1)S(1)}, u32[]{:S(2)}, u32[]{:S(2)}) collective-permute-start(bf16[2,64,2048]{2,1,0:T(8,128)(2,1)S(1)} %pad_maximum_fusion.24), channel_id=1, source_target_pairs={{8,16},{9,17},{10,18},{11,19},{12,20},{13,21},{14,22},{15,23},{16,... | collective-permute-start | bytes 1572872 | tf_op jit(solution)/shard_map/ppermute | solution.py:119
  651.8 63.1 %collective-permute-start.73 = (f32[16,64,512]{2,1,0:T(8,128)}, f32[16,64,512]{2,1,0:T(8,128)}, u32[]{:S(2)}, u32[]{:S(2)}) collective-permute-start(f32[16,64,512]{2,1,0:T(8,128)} %dynamic-slice_bitcast_fusion.1), channel_id=1, source_target_pairs={{0,1},{1,0},{2,3},{3,2},{4,5},{5,4},{6,7},{7,6},{8,9},{9,8},{10,11... | collective-permute-start | bytes 6291464 | tf_op jit(solution)/shard_map/ppermute | solution.py:116
  690.0 29.4 %collective-permute-start.72 = (f32[16,64,512]{2,1,0:T(8,128)}, f32[16,64,512]{2,1,0:T(8,128)}, u32[]{:S(2)}, u32[]{:S(2)}) collective-permute-start(f32[16,64,512]{2,1,0:T(8,128)} %dynamic-slice_bitcast_fusion.2), channel_id=1, source_target_pairs={{0,1},{1,0},{2,3},{3,2},{4,5},{5,4},{6,7},{7,6},{8,9},{9,8},{10,11... | collective-permute-start | bytes 6291464 | tf_op jit(solution)/shard_map/ppermute | solution.py:116
  701.5 20.9 %all-to-all-start.1 = ((bf16[128,8,256]{0,2,1:T(8,128)(2,1)}), bf16[128,8,256]{0,2,1:T(8,128)(2,1)S(1)}, u32[]{:S(2)}, u32[]{:S(2)}) async-start(bf16[128,8,256]{0,2,1:T(8,128)(2,1)} %bitcast.110), calls=%async_computation.1 | async-start | bytes 1048576 | tf_op jit(solution)/shard_map/all_to_all | solution.py:438
  705.7 170.3 %all-gather.9.cloned.1.call-start = ((), (), s32[]{:S(2)}) async-start(), calls=%async_computation.9 | async-start | bytes 4718592 | tf_op jit(solution)/shard_map/all_gather | solution.py:153
  714.9 137.8 %collective-permute-start.64 = (bf16[512,512]{1,0:T(8,128)(2,1)}, bf16[512,512]{1,0:T(8,128)(2,1)}, u32[]{:S(2)}, u32[]{:S(2)}) collective-permute-start(bf16[512,512]{1,0:T(8,128)(2,1)} %param.20), channel_id=1, source_target_pairs={{0,2},{1,3},{2,0},{3,1},{4,6},{5,7},{6,4},{7,5},{8,10},{9,11},{10,... | collective-permute-start | bytes 1572872 | tf_op jit(solution)/shard_map/ppermute | solution.py:116
  719.4 70.0 %collective-permute-start.74 = (f32[256,2048]{1,0:T(8,128)}, f32[256,2048]{1,0:T(8,128)}, u32[]{:S(2)}, u32[]{:S(2)}) collective-permute-start(f32[256,2048]{1,0:T(8,128)} %dynamic-slice_bitcast_fusion), channel_id=1, source_target_pairs={{0,1},{1,0},{2,3},{3,2},{4,5},{5,4},{6,7},{7,6},{8,9},{9,8},{10,11... | collective-permute-start | bytes 6291464 | tf_op jit(solution)/shard_map/ppermute | solution.py:116
  722.4 49.3 %all-to-all-start.6 = ((bf16[16,64,512]{2,1,0:T(8,128)(2,1)}), bf16[16,64,512]{2,1,0:T(8,128)(2,1)S(1)}, u32[]{:S(2)}, u32[]{:S(2)}) async-start(bf16[16,64,512]{2,1,0:T(8,128)(2,1)} %fusion.27), calls=%async_computation.6 | async-start | bytes 2097152 | tf_op jit(solution)/shard_map/all_to_all | solution.py:428
  771.7 57.3 %all-to-all-start.5 = ((bf16[16,64,512]{2,1,0:T(8,128)(2,1)}), bf16[16,64,512]{2,1,0:T(8,128)(2,1)S(1)}, u32[]{:S(2)}, u32[]{:S(2)}) async-start(bf16[16,64,512]{2,1,0:T(8,128)(2,1)} %fusion.28), calls=%async_computation.5 | async-start | bytes 2097152 | tf_op jit(solution)/shard_map/all_to_all | solution.py:428
  789.3 63.4 %collective-permute-start.62 = (bf16[512,2048]{1,0:T(8,128)(2,1)}, bf16[512,2048]{1,0:T(8,128)(2,1)}, u32[]{:S(2)}, u32[]{:S(2)}) collective-permute-start(bf16[512,2048]{1,0:T(8,128)(2,1)} %param.18), channel_id=1, source_target_pairs={{0,2},{1,3},{2,0},{3,1},{4,6},{5,7},{6,4},{7,5},{8,10},{9,11},{10,... | collective-permute-start | bytes 6291464 | tf_op jit(solution)/shard_map/ppermute | solution.py:116
  829.0 21.0 %all-to-all-start.2 = ((bf16[8,128,384]{2,1,0:T(8,128)(2,1)}), bf16[8,128,384]{2,1,0:T(8,128)(2,1)S(1)}, u32[]{:S(2)}, u32[]{:S(2)}) async-start(bf16[8,128,384]{2,1,0:T(8,128)(2,1)} %bitcast.513), calls=%async_computation.2 | async-start | bytes 1572864 | tf_op jit(solution)/shard_map/all_to_all | solution.py:485
  850.7 15.0 %collective-permute-start.59 = (bf16[512,2048]{1,0:T(8,128)(2,1)}, bf16[512,2048]{1,0:T(8,128)(2,1)S(1)}, u32[]{:S(2)}, u32[]{:S(2)}) collective-permute-start(bf16[512,2048]{1,0:T(8,128)(2,1)} %param.18), channel_id=1, source_target_pairs={{0,1},{1,0},{2,3},{3,2},{4,5},{5,4},{6,7},{7,6},{8,9},{9,8},{10,11... | collective-permute-start | bytes 6291464 | tf_op jit(solution)/shard_map/ppermute | solution.py:116
  852.8 13.7 %collective-permute-start.65 = (bf16[512,2048]{1,0:T(8,128)(2,1)}, bf16[512,2048]{1,0:T(8,128)(2,1)S(1)}, u32[]{:S(2)}, u32[]{:S(2)}) collective-permute-start(bf16[512,2048]{1,0:T(8,128)(2,1)} %collective-permute-done.62), channel_id=1, source_target_pairs={{0,1},{1,0},{2,3},{3,2},{4,5},{5,4},{6,7},{7,6},{8,9},{9,8},{10,11... | collective-permute-start | bytes 6291464 | tf_op jit(solution)/shard_map/ppermute | solution.py:116
  874.4 20.2 %collective-permute-start.69 = (f32[8,64,384]{2,1,0:T(8,128)}, f32[8,64,384]{2,1,0:T(8,128)S(1)}, u32[]{:S(2)}, u32[]{:S(2)}) collective-permute-start(f32[8,64,384]{2,1,0:T(8,128)} %dynamic-slice_bitcast_fusion.5), channel_id=1, source_target_pairs={{0,2},{1,3},{2,0},{3,1},{4,6},{5,7},{6,4},{7,5},{8,10},{9,11},{10,... | collective-permute-start | bytes 2359304 | tf_op jit(solution)/shard_map/ppermute | solution.py:116
  880.6 26.9 %collective-permute-start.70 = (f32[2,64,2048]{2,1,0:T(8,128)}, f32[2,64,2048]{2,1,0:T(8,128)}, u32[]{:S(2)}, u32[]{:S(2)}) collective-permute-start(f32[2,64,2048]{2,1,0:T(8,128)} %dynamic-slice_bitcast_fusion.4), channel_id=1, source_target_pairs={{0,1},{1,0},{2,3},{3,2},{4,5},{5,4},{6,7},{7,6},{8,9},{9,8},{10,11... | collective-permute-start | bytes 3145736 | tf_op jit(solution)/shard_map/ppermute | solution.py:116
  881.5 15.3 %all-to-all-start.3 = ((f32[32,1,128]{2,1,0:T(1,128)}), f32[32,1,128]{2,1,0:T(1,128)S(1)}, u32[]{:S(2)}, u32[]{:S(2)}) async-start(f32[32,1,128]{2,1,0:T(1,128)} %reshape.599), calls=%async_computation.3 | async-start | bytes 32768 | tf_op jit(solution)/shard_map/all_to_all | solution.py:509
  896.7 23.4 %all-to-all-start.4 = ((f32[8,64,384]{2,1,0:T(8,128)}), f32[8,64,384]{2,1,0:T(8,128)S(1)}, u32[]{:S(2)}, u32[]{:S(2)}) async-start(f32[8,64,384]{2,1,0:T(8,128)} %bitcast_add_fusion.5), calls=%async_computation.4 | async-start | bytes 1572864 | tf_op jit(solution)/shard_map/all_to_all | solution.py:503
  (102 other events, 1924.2 us)
Sparse Core Ops, SparseCore 0:
  10.8 103.8 all-gather.6
  117.5 94.0 all-gather.4
  722.5 110.0 all-gather.8
